TPU v7x, 256 devices: a whole 4x4x8 slice. The times are simulated.
256 devices in a mesh: rep: 8 (over z_lo, x), exp: 32 (over y, z_hi, core).
Axes of the slice: x: 4, y: 4, z: 8 (z_hi: 4, z_lo: 2; z = z_hi * 2 + z_lo), core: 2. Of those that a mesh axis runs over, the one named last changes fastest.
Arguments:
- hidden: bfloat16 [4096, 7168], P(('rep', 'exp')), may hold values from -6 to 6
- expert_ids: int32 [4096, 8], P(('rep', 'exp')), may hold values from 0 to 15, all different within a row; in each aligned block of 16 rows (0 to 15, 16 to 31, ...) at most 10 rows name the same one
- router: bfloat16 [7168, 16], replicated, may hold values from -0.0625 to 0.0625
- gate_up: bfloat16 [32, 512, 2, 7168], P('exp', 'rep'), may hold values from -0.0625 to 0.0625
- down_weight: bfloat16 [32, 512, 7168], P('exp', 'rep'), may hold values from -0.1875 to 0.1875
- query_latent: bfloat16 [4096, 64, 512], P(('rep', 'exp')), may hold values from -110 to 110
- query_rope: bfloat16 [4096, 64, 64], P(('rep', 'exp')), may hold values from -6 to 6
- cache_latent: bfloat16 [4096, 256, 512], P(('rep', 'exp')), may hold values from -8 to 8
- cache_rope: bfloat16 [4096, 64, 256], P(('rep', 'exp')), may hold values from -5 to 5
- lengths: int32 [4096], P(('rep', 'exp')), may hold values from 32 to 256, as said below
Outputs:
- moe_out: bfloat16 [4096, 7168], P(('rep', 'exp'))
- attn_latent: bfloat16 [4096, 64, 512], P(('rep', 'exp'))
Inputs may be any that keep to these rules, and one draw needn't show every extreme that they name: `expert_ids`: in every aligned block of 16 rows no expert is named by more than 10 pairs, a bound that some block reaches. `lengths`: some row has length 256.
All inputs are finite; a program needn't handle non-finite values.
Results may differ from a plain program's by a relative error of at most 0.015.
Values may be sent and summed in bfloat16 or wider, within the bound.
No kernel may reach another device: no remote copies, remote signals or barrier semaphores. Data moves between devices by JAX's collectives and lax.ppermute only.
A program may use at most 128 MiB of HBM per device.

v0:
```python
import functools
import math

import jax
import jax.numpy as jnp
from jax import lax
from jax.experimental import pallas as pl
from jax.experimental.pallas import tpu as pltpu
from jax.sharding import Mesh
from jax.sharding import PartitionSpec as P

ROPE = 64
NOPE = 128
ROUTE_SCALE = 2.827
AXES = ("zl", "x", "y", "zh", "c")
SIZES = (2, 4, 4, 4, 2)
ROWS_OF = ("y", "zh", "zl", "c")
NX, NY, NZ, NC = 4, 4, 8, 2
N_EXPERTS = 16


def index_of(x, y, z, c):
    return (((z % 2) * NX + x) * NY + y) * (NZ // 2) * NC + (z // 2) * NC + c


def shift(value, x=0, y=0, z=0, c=0):
    pairs = []
    for i in range(NX):
        for j in range(NY):
            for k in range(NZ):
                for m in range(NC):
                    pairs.append(
                        (
                            index_of(i, j, k, m),
                            index_of((i + x) % NX, (j + y) % NY, (k + z) % NZ, (m + c) % NC),
                        )
                    )
    return lax.ppermute(value, AXES, pairs)


def exchange_sum(blocks, axis):
    got = lax.all_to_all(blocks, axis, split_axis=0, concat_axis=0, tiled=True)
    return jnp.sum(got.astype(jnp.float32), axis=0).astype(jnp.bfloat16)


def attend(query_latent, query_rope, cache_latent, cache_rope, row_lengths):
    score_scale = 1.0 / math.sqrt(NOPE + ROPE)
    scores = jnp.einsum(
        "rhc,rlc->rhl", query_latent, cache_latent, preferred_element_type=jnp.float32
    )
    scores = scores + jnp.einsum(
        "rhp,rpl->rhl", query_rope, cache_rope, preferred_element_type=jnp.float32
    )
    scores = scores * score_scale
    valid_mask = (
        jnp.arange(cache_latent.shape[1], dtype=jnp.int32)[None, None, :]
        < row_lengths[:, None, None]
    )
    scores = jnp.where(valid_mask, scores, -1e30)
    row_max = jnp.max(scores, axis=2, keepdims=True)
    weights_raw = jnp.where(valid_mask, jnp.exp(scores - row_max), 0.0)
    attn_probs = (weights_raw / jnp.sum(weights_raw, axis=2, keepdims=True)).astype(jnp.bfloat16)
    output = jnp.einsum(
        "rhl,rlc->rhc", attn_probs, cache_latent, preferred_element_type=jnp.float32
    )
    return output.astype(jnp.bfloat16)


def mixing_table(hidden, expert_ids, router):
    logits = jnp.dot(hidden, router, preferred_element_type=jnp.float32)
    experts = router.shape[1]
    named = jnp.any(
        expert_ids[:, :, None] == jnp.arange(experts, dtype=jnp.int32)[None, None, :], axis=1
    )
    gates = jnp.where(named, jax.nn.sigmoid(logits), 0.0)
    return gates / jnp.sum(gates, axis=1, keepdims=True) * ROUTE_SCALE


def hidden_kernel(expert_ref, x_ref, *refs):
    pieces, (out_ref, weights, sems) = refs[:-3], refs[-3:]
    gates, width = weights.shape[0] // 2, weights.shape[1]
    units = gates // NX
    experts = N_EXPERTS

    @pl.when(pl.program_id(0) == 0)
    def _():
        copies = []
        for kind in range(2):
            for shard in range(NX):
                piece = kind * NX + shard
                target = weights.at[pl.ds(piece * units, units), :]
                copies.append(pltpu.make_async_copy(pieces[piece], target, sems.at[piece]))
        for copy in copies:
            copy.start()
        for copy in copies:
            copy.wait()

    both = lax.dot_general(
        x_ref[:, :width],
        weights[...],
        (((1,), (1,)), ((), ())),
        preferred_element_type=jnp.float32,
    )
    table = x_ref[:, width:].astype(jnp.float32)
    lane = lax.broadcasted_iota(jnp.int32, table.shape, 1)
    picked = ((lane & (experts - 1)) == expert_ref[0]) & (lane < 2 * experts)
    scale = jnp.sum(jnp.where(picked, table, 0.0), axis=1, keepdims=True)
    gate, up = both[:, :gates], both[:, gates:]
    acts = (gate / (1.0 + jnp.exp(-gate)) * up * scale).astype(jnp.bfloat16)
    blocks = acts.shape[0] // 32
    acts = acts.reshape(blocks, 2, 16, gates)
    for c in range(NC):
        out_ref[c] = acts[:, c].reshape(blocks * 16, gates)


def hidden_units(everyone, pieces, expert):
    count, wide = everyone.shape
    gates, width = NX * pieces[-1].shape[0], pieces[-1].shape[1]
    block = 256
    return pl.pallas_call(
        hidden_kernel,
        out_shape=jax.ShapeDtypeStruct((NC, count // NC, gates), jnp.bfloat16),
        grid_spec=pltpu.PrefetchScalarGridSpec(
            num_scalar_prefetch=1,
            grid=(count // block,),
            in_specs=[pl.BlockSpec((block, wide), lambda i, e: (i, 0))]
            + [pl.BlockSpec(memory_space=pltpu.HBM)] * len(pieces),
            out_specs=pl.BlockSpec((NC, block // NC, gates), lambda i, e: (0, i, 0)),
            scratch_shapes=[
                pltpu.VMEM((2 * gates, width), jnp.bfloat16),
                pltpu.SemaphoreType.DMA((2 * NX,)),
            ],
        ),
        compiler_params=pltpu.CompilerParams(vmem_limit_bytes=44 << 20),
        cost_estimate=pl.CostEstimate(
            flops=4 * count * gates * width,
            bytes_accessed=2 * (count * wide + 2 * gates * width),
            transcendentals=count * gates,
        ),
        name="hidden_units",
    )(jnp.reshape(expert, (1,)).astype(jnp.int32), everyone, *pieces)


def down_kernel(turn, place_ref, mine_ref, recv_ref, own_ref, twin_ref, out_ref, acts):
    gates = own_ref.shape[0]

    @pl.when(pl.program_id(0) == 0)
    def _():
        if not turn:
            acts[:, :gates] = mine_ref[0]
            acts[:, gates:] = recv_ref[...]
        else:
            rows = mine_ref.shape[1] // (NY * NZ)
            for z in range(NZ):
                for y in range(NY):
                    source = pl.ds((y * NZ + z) * rows, rows)
                    target = pl.ds((z * NY + y) * rows, rows)
                    acts[target, :gates] = mine_ref[0, source, :]
                    acts[target, gates:] = recv_ref[source, :]

    out = jnp.dot(acts[:, :gates], own_ref[...], preferred_element_type=jnp.float32)
    out = out + jnp.dot(acts[:, gates:], twin_ref[...], preferred_element_type=jnp.float32)
    out_ref[...] = out.astype(jnp.bfloat16)


def project(acts, recv, own, twin, place, first, span, turn):
    _, count, gates = acts.shape
    block = 512
    skip = first // block
    return pl.pallas_call(
        functools.partial(down_kernel, turn),
        out_shape=jax.ShapeDtypeStruct((count, span), jnp.bfloat16),
        grid_spec=pltpu.PrefetchScalarGridSpec(
            num_scalar_prefetch=1,
            grid=(span // block,),
            in_specs=[
                pl.BlockSpec((1, count, gates), lambda i, p: (p[0], 0, 0)),
                pl.BlockSpec((count, gates), lambda i, p: (0, 0)),
                pl.BlockSpec((gates, block), lambda i, p: (0, i + skip)),
                pl.BlockSpec((gates, block), lambda i, p: (0, i + skip)),
            ],
            out_specs=pl.BlockSpec((count, block), lambda i, p: (0, i)),
            scratch_shapes=[pltpu.VMEM((count, 2 * gates), jnp.bfloat16)],
        ),
        compiler_params=pltpu.CompilerParams(vmem_limit_bytes=(56 if turn else 16) << 20),
        cost_estimate=pl.CostEstimate(
            flops=4 * count * gates * span,
            bytes_accessed=2 * (2 * gates * span + count * span + 2 * count * gates),
            transcendentals=0,
        ),
        name="project",
    )(place, acts, recv, own, twin)


def on_device(
    hidden,
    expert_ids,
    router,
    gate_up,
    down_weight,
    query_latent,
    query_rope,
    cache_latent,
    cache_rope,
    lengths,
):
    rows, width = hidden.shape
    units = gate_up.shape[1]
    experts = router.shape[1]
    cut = width // 7 * 3
    core = lax.axis_index("c")
    place = jnp.reshape(core, (1,)).astype(jnp.int32)
    expert = lax.axis_index("y") * (NZ // 2) + lax.axis_index("zh")

    mixing = mixing_table(hidden, expert_ids, router)
    high = lax.reduce_precision(mixing, 8, 7)
    low = mixing - high
    table = jnp.concatenate([high, low], axis=1).astype(jnp.bfloat16)
    table = jnp.pad(table, ((0, 0), (0, 128 - 2 * experts)))
    everyone = lax.all_gather(
        jnp.concatenate([hidden, table], axis=1), ROWS_OF, axis=0, tiled=True
    )
    count = everyone.shape[0]

    attn_latent = attend(query_latent, query_rope, cache_latent, cache_rope, lengths)

    own = gate_up[0].transpose(1, 0, 2)
    gate, up = own[0], own[1]
    gate_left, up_left = shift(gate, x=1), shift(up, x=1)
    gate_right, up_right = shift(gate, x=-1), shift(up, x=-1)
    gate_far, up_far = shift(gate_left, x=1), shift(up_right, x=-1)

    down = down_weight[0]
    down_left, down_right = shift(down, x=1), shift(down, x=-1)
    half = units // 2
    far = [shift(down_left[:half], x=1), shift(down_right[half:], x=-1)]
    down = jnp.concatenate([down, down_left, down_right] + far, axis=0)
    twin = shift(down, c=1)

    pieces = [gate, gate_left, gate_right, gate_far, up, up_left, up_right, up_far]
    acts = hidden_units(everyone, pieces, expert)
    recv = shift(lax.dynamic_index_in_dim(acts, 1 - core, axis=0, keepdims=False), c=1)

    out_b = project(acts, recv, down, twin, place, cut, width - cut, True)
    out_b = lax.psum_scatter(out_b, ("zh", "zl"), scatter_dimension=0, tiled=True)
    out_a = project(acts, recv, down, twin, place, 0, cut, False)
    out_a = exchange_sum(out_a.reshape(NY, NZ * rows, cut), "y")
    out_a, out_b = lax.optimization_barrier((out_a, out_b))
    out_a = exchange_sum(out_a.reshape(NZ, rows, cut), ("zh", "zl"))
    out_b = exchange_sum(out_b.reshape(NY, rows, width - cut), "y")
    moe_out = jnp.concatenate([out_a, out_b], axis=1)

    return (moe_out, attn_latent)


def solution(mesh):
    parts = Mesh(mesh.devices.reshape(SIZES), AXES)
    rep, exp = ("zl", "x"), ("y", "zh", "c")
    return jax.shard_map(
        on_device,
        mesh=parts,
        in_specs=(
            P(AXES, None),
            P(AXES, None),
            P(),
            P(exp, rep, None, None),
            P(exp, rep, None),
            P(AXES, None, None),
            P(AXES, None, None),
            P(AXES, None, None),
            P(AXES, None, None),
            P(AXES),
        ),
        out_specs=(P(AXES, None), P(AXES, None, None)),
        check_vma=False,
    )
```

profile of v0, /device:TPU:2, one launch (start us, length us, event | category | flops | bytes accessed | tf_op | source)
XLA Modules:
  0.0 243.7 jit_solution(2355192692835558594)
XLA Ops:
  7.2 0.9 copy.14
  8.2 1.4 fusion.18
  9.8 1.7 pad_maximum_fusion
  11.5 1.6 collective-permute-start.7
  14.0 1.8 copy.17
  15.8 1.0 constant_dynamic-update-slice_fusion.4
  16.8 17.1 %collective-permute-done.7 = bf16[64,7168]{1,0:T(8,128)(2,1)S(1)} collective-permute-done((bf16[64,7168]{1,0:T(8,128)(2,1)}, bf16[64,7168]{1,0:T(8,128)(2,1)S(1)}, u32[]{:S(2)}, u32[]{:S(2)}) %collective-permute-start.7) | collective-permute-done | bytes 917536 | tf_op jit(solution)/shard_map/ppermute | solution.py:38
  33.9 1.6 collective-permute-start.9
  36.1 1.0 constant_dynamic-update-slice_fusion.3
  37.1 1.0 constant_dynamic-update-slice_fusion.2
  38.1 7.1 %collective-permute-done.9 = bf16[32,7168]{1,0:T(8,128)(2,1)S(1)} collective-permute-done((bf16[32,7168]{1,0:T(8,128)(2,1)S(1)}, bf16[32,7168]{1,0:T(8,128)(2,1)S(1)}, u32[]{:S(2)}, u32[]{:S(2)}) %collective-permute-start.9) | collective-permute-done | bytes 458784 | tf_op jit(solution)/shard_map/ppermute | solution.py:38
  47.7 1.3 collective-permute-start
  49.9 2.2 collective-permute-start.1
  52.1 19.0 %collective-permute-done.refs_1_ = bf16[64,7168]{1,0:T(8,128)(2,1)} collective-permute-done((bf16[64,7168]{1,0:T(8,128)(2,1)S(1)}, bf16[64,7168]{1,0:T(8,128)(2,1)}, u32[]{:S(2)}, u32[]{:S(2)}) %collective-permute-start) | collective-permute-done | bytes 917536 | tf_op jit(solution)/shard_map/ppermute | solution.py:38
  71.1 1.2 collective-permute-start.2
  72.3 1.0 collective-permute-start.5
  73.3 18.6 %collective-permute-done.1.refs_2_ = bf16[64,7168]{1,0:T(8,128)(2,1)} collective-permute-done((bf16[64,7168]{1,0:T(8,128)(2,1)S(1)}, bf16[64,7168]{1,0:T(8,128)(2,1)}, u32[]{:S(2)}, u32[]{:S(2)}) %collective-permute-start.1) | collective-permute-done | bytes 917536 | tf_op jit(solution)/shard_map/ppermute | solution.py:38
  92.0 18.0 %collective-permute-done.2.refs_3_ = bf16[64,7168]{1,0:T(8,128)(2,1)} collective-permute-done((bf16[64,7168]{1,0:T(8,128)(2,1)}, bf16[64,7168]{1,0:T(8,128)(2,1)}, u32[]{:S(2)}, u32[]{:S(2)}) %collective-permute-start.2) | collective-permute-done | bytes 917536 | tf_op jit(solution)/shard_map/ppermute | solution.py:38
  110.0 0.9 collective-permute-done.5.refs_7_
  110.9 13.6 %hidden_units.1.mine_ref = bf16[2,512,256]{2,1,0:T(8,128)(2,1)S(1)} custom-call(s32[1]{0:T(128)} %bitcast.1.expert_ref, bf16[1024,7296]{1,0:T(8,128)(2,1)} %all-gather.2.cloned.1.call-done.x_ref, bf16[64,7168]{1,0:T(8,128)(2,1)S(1)} %get-tuple-element.7.refs_0_, bf16[64,7168]{1,0:T(8,128)(2,1)} %collective-permute-done.refs_1_, ...), custom_call_target="tpu_custom_call" | custom-call | flops 7516192768 | bytes 22282240 | tf_op jit(solution)/shard_map/hidden_units/pallas_call | solution.py:120
  124.9 1.5 collective-permute-done.6.recv_ref
  127.1 8.4 %project.3 = bf16[512,4096]{1,0:T(8,128)(2,1)} custom-call(s32[1]{0:T(128)} %bitcast.place_ref, bf16[2,512,256]{2,1,0:T(8,128)(2,1)} %copy-done.1, bf16[512,256]{1,0:T(8,128)(2,1)} %copy-done.3, bf16[256,7168]{1,0:T(8,128)(2,1)} %constant_dynamic-update-slice_fusion.own_ref, bf16[256,7168]{1,0:T(8,128)(2,1)} %collective-permute-done.11.twin_ref), custom_call_target="tpu_custom_call" | custom-call | flops 2147483648 | bytes 8912896 | tf_op jit(solution)/shard_map/project/pallas_call | solution.py:170
  135.5 1.0 copy-done.2
  136.6 5.1 %project.2 = bf16[512,3072]{1,0:T(8,128)(2,1)S(1)} custom-call(s32[1]{0:T(128)} %bitcast.place_ref, bf16[2,512,256]{2,1,0:T(8,128)(2,1)S(1)} %copy-done.2, bf16[512,256]{1,0:T(8,128)(2,1)S(1)} %copy-done.4, bf16[256,7168]{1,0:T(8,128)(2,1)} %constant_dynamic-update-slice_fusion.own_ref, bf16[256,7168]{1,0:T(8,128)(2,1)} %collective-permute-done.11.twin_ref), custom_call_target="tpu_custom_call" | custom-call | flops 1610612736 | bytes 6815744 | tf_op jit(solution)/shard_map/project/pallas_call | solution.py:170
  141.7 43.3 %all_to_all.15 = bf16[4,128,3072]{2,1,0:T(8,128)(2,1)} all-to-all(bf16[4,128,3072]{2,1,0:T(8,128)(2,1)S(1)} %bitcast.27), channel_id=1, replica_groups=mesh['zl'=2,'x'=4,'y'=4,'zh'=4,'c'=2] {'y'}, dimensions={0} | all-to-all | bytes 6291456 | tf_op jit(solution)/shard_map/all_to_all | solution.py:42
  185.0 3.6 %reduce_sum.55 = bf16[128,3072]{1,0:T(8,128)(2,1)} reduce(bf16[4,128,3072]{2,1,0:T(8,128)(2,1)} %all_to_all.15, bf16[]{:T(256)} %constant.35.clone.1), dimensions={0}, to_apply=%region_2.3 | reduce | flops 1179648 | bytes 3932162 | tf_op jit(solution)/shard_map/reduce_sum | solution.py:43
  188.6 7.3 %reduce-scatter.2.cloned.1.call-done = bf16[64,4096]{1,0:T(8,128)(2,1)} async-done(((bf16[512,4096]{1,0:T(8,128)(2,1)}), bf16[64,4096]{1,0:T(8,128)(2,1)}) %reduce-scatter.2.cloned.1.call-update) | async-done | bytes 524304 | tf_op jit(solution)/shard_map/reduce_scatter | solution.py:245
  195.9 13.8 %all_to_all.16 = bf16[4,16,4096]{2,1,0:T(8,128)(2,1)S(1)} all-to-all(bf16[4,16,4096]{2,1,0:T(8,128)(2,1)} %bitcast.31), channel_id=1, replica_groups=mesh['zl'=2,'x'=4,'y'=4,'zh'=4,'c'=2] {'y'}, dimensions={0} | all-to-all | bytes 1048576 | tf_op jit(solution)/shard_map/all_to_all | solution.py:42
  209.7 4.4 %all-to-all-start.1 = ((bf16[8,16,3072]{2,1,0:T(8,128)(2,1)}), bf16[8,16,3072]{2,1,0:T(8,128)(2,1)S(1)}, u32[]{:S(2)}, u32[]{:S(2)}) async-start(bf16[8,16,3072]{2,1,0:T(8,128)(2,1)} %bitcast.10), calls=%async_computation.2 | async-start | bytes 1572864 | tf_op jit(solution)/shard_map/all_to_all | solution.py:42
  214.2 3.6 %fusion.20 = f32[16,64,256]{2,1,0:T(8,128)S(1)} fusion(bf16[16,64,512]{2,1,0:T(8,128)(2,1)S(1)} %copy-done, bf16[16,256,512]{2,1,0:T(8,128)(2,1)} %param.17), kind=kOutput, calls=%fused_computation.41 | convolution fusion | flops 268435456 | bytes 6291456 | tf_op jit(solution)/shard_map/rhc,rlc->rhl/dot_general | solution.py:48
  218.5 5.1 %convolution_convert_fusion = bf16[16,64,512]{2,1,0:T(8,128)(2,1)} fusion(bf16[16,256,512]{2,1,0:T(8,128)(2,1)} %param.17, f32[16,64]{1,0:T(8,128)S(1)} %fusion.19, f32[16,64,256]{2,1,0:T(8,128)S(1)} %fusion.5, pred[16,256]{1,0:T(8,128)(4,1)S(1)} %iota_compare_fusion.1), kind=kOutput, calls=%fused_computation.3 | convolution fusion | flops 270009600 | bytes 6299648 | tf_op jit(solution)/shard_map/rhl,rlc->rhc/dot_general | solution.py:63
  223.7 12.4 %all-to-all-done.1 = bf16[8,16,3072]{2,1,0:T(8,128)(2,1)S(1)} async-done(((bf16[8,16,3072]{2,1,0:T(8,128)(2,1)}), bf16[8,16,3072]{2,1,0:T(8,128)(2,1)S(1)}, u32[]{:S(2)}, u32[]{:S(2)}) %all-to-all-start.1) | async-done | bytes 786464 | tf_op jit(solution)/shard_map/all_to_all | solution.py:42
  (48 shorter events, 8.1 us)
Async XLA Ops:
  7.2 207.0 %copy-start = (bf16[16,64,512]{2,1,0:T(8,128)(2,1)S(1)}, bf16[16,64,512]{2,1,0:T(8,128)(2,1)}, u32[]{:S(2)}) copy-start(bf16[16,64,512]{2,1,0:T(8,128)(2,1)} %param.15) | copy-start | bytes 3145732
  7.2 8.6 %copy-start.5 = (bf16[1,64,7168]{2,1,0:T(8,128)(2,1)S(1)}, bf16[1,64,7168]{2,1,0:T(8,128)(2,1)}, u32[]{:S(2)}) copy-start(bf16[1,64,7168]{2,1,0:T(8,128)(2,1)} %param.14) | copy-start | bytes 2752516
  7.2 103.7 %all-gather.2.cloned.1.call-start = ((), (), s32[]{:S(2)}) async-start(), calls=%async_computation.4 | async-start | bytes 15175680 | tf_op jit(solution)/shard_map/all_gather | solution.py:220
  11.5 184.5 %reduce-scatter.2.cloned.1.call-start = ((), (), s32[]{:S(2)}) async-start(), calls=%async_computation.5 | async-start | bytes 4718592 | tf_op jit(solution)/shard_map/reduce_scatter | solution.py:245
  11.5 22.4 %collective-permute-start.7 = (bf16[64,7168]{1,0:T(8,128)(2,1)}, bf16[64,7168]{1,0:T(8,128)(2,1)S(1)}, u32[]{:S(2)}, u32[]{:S(2)}) collective-permute-start(bf16[64,7168]{1,0:T(8,128)(2,1)} %bitcast.29), channel_id=1, source_target_pairs={{0,32},{1,33},{128,160},{129,161},{2,34},{3,35},{130,162},{131,163... | collective-permute-start | bytes 2752520 | tf_op jit(solution)/shard_map/ppermute | solution.py:38
  13.1 22.4 %collective-permute-start.8 = (bf16[64,7168]{1,0:T(8,128)(2,1)}, bf16[64,7168]{1,0:T(8,128)(2,1)S(1)}, u32[]{:S(2)}, u32[]{:S(2)}) collective-permute-start(bf16[64,7168]{1,0:T(8,128)(2,1)} %bitcast.30), channel_id=1, source_target_pairs={{0,96},{1,97},{128,224},{129,225},{2,98},{3,99},{130,226},{131,227... | collective-permute-start | bytes 2752520 | tf_op jit(solution)/shard_map/ppermute | solution.py:38
  33.9 11.3 %collective-permute-start.9 = (bf16[32,7168]{1,0:T(8,128)(2,1)S(1)}, bf16[32,7168]{1,0:T(8,128)(2,1)S(1)}, u32[]{:S(2)}, u32[]{:S(2)}) collective-permute-start(bf16[32,7168]{1,0:T(8,128)(2,1)S(1)} %slice.18), channel_id=1, source_target_pairs={{0,32},{1,33},{128,160},{129,161},{2,34},{3,35},{130,162},{131,163... | collective-permute-start | bytes 1376264 | tf_op jit(solution)/shard_map/ppermute | solution.py:38
  35.5 11.3 %collective-permute-start.10 = (bf16[32,7168]{1,0:T(8,128)(2,1)S(1)}, bf16[32,7168]{1,0:T(8,128)(2,1)S(1)}, u32[]{:S(2)}, u32[]{:S(2)}) collective-permute-start(bf16[32,7168]{1,0:T(8,128)(2,1)S(1)} %slice.19), channel_id=1, source_target_pairs={{0,96},{1,97},{128,224},{129,225},{2,98},{3,99},{130,226},{131,227... | collective-permute-start | bytes 1376264 | tf_op jit(solution)/shard_map/ppermute | solution.py:38
  47.6 77.2 %collective-permute-start.11 = (bf16[256,7168]{1,0:T(8,128)(2,1)}, bf16[256,7168]{1,0:T(8,128)(2,1)}, u32[]{:S(2)}, u32[]{:S(2)}) collective-permute-start(bf16[256,7168]{1,0:T(8,128)(2,1)} %constant_dynamic-update-slice_fusion.own_ref), channel_id=1, source_target_pairs={{0,1},{1,0},{128,129},{129,128},{2,3},{3,2},{130,131},{131,130},{4... | collective-permute-start | bytes 11010056 | tf_op jit(solution)/shard_map/ppermute | solution.py:38
  47.7 23.3 %collective-permute-start = (bf16[64,7168]{1,0:T(8,128)(2,1)S(1)}, bf16[64,7168]{1,0:T(8,128)(2,1)}, u32[]{:S(2)}, u32[]{:S(2)}) collective-permute-start(bf16[64,7168]{1,0:T(8,128)(2,1)S(1)} %get-tuple-element.7.refs_0_), channel_id=1, source_target_pairs={{0,32},{1,33},{128,160},{129,161},{2,34},{3,35},{130,162},{131,163... | collective-permute-start | bytes 2752520 | tf_op jit(solution)/shard_map/ppermute | solution.py:38
  49.0 23.3 %collective-permute-start.4 = (bf16[64,7168]{1,0:T(8,128)(2,1)S(1)}, bf16[64,7168]{1,0:T(8,128)(2,1)}, u32[]{:S(2)}, u32[]{:S(2)}) collective-permute-start(bf16[64,7168]{1,0:T(8,128)(2,1)S(1)} %get-tuple-element.6.refs_4_), channel_id=1, source_target_pairs={{0,96},{1,97},{128,224},{129,225},{2,98},{3,99},{130,226},{131,227... | collective-permute-start | bytes 2752520 | tf_op jit(solution)/shard_map/ppermute | solution.py:38
  49.9 42.1 %collective-permute-start.1 = (bf16[64,7168]{1,0:T(8,128)(2,1)S(1)}, bf16[64,7168]{1,0:T(8,128)(2,1)}, u32[]{:S(2)}, u32[]{:S(2)}) collective-permute-start(bf16[64,7168]{1,0:T(8,128)(2,1)S(1)} %get-tuple-element.7.refs_0_), channel_id=1, source_target_pairs={{0,96},{1,97},{128,224},{129,225},{2,98},{3,99},{130,226},{131,227... | collective-permute-start | bytes 2752520 | tf_op jit(solution)/shard_map/ppermute | solution.py:38
  52.1 39.9 %collective-permute-start.3 = (bf16[64,7168]{1,0:T(8,128)(2,1)S(1)}, bf16[64,7168]{1,0:T(8,128)(2,1)}, u32[]{:S(2)}, u32[]{:S(2)}) collective-permute-start(bf16[64,7168]{1,0:T(8,128)(2,1)S(1)} %get-tuple-element.6.refs_4_), channel_id=1, source_target_pairs={{0,32},{1,33},{128,160},{129,161},{2,34},{3,35},{130,162},{131,163... | collective-permute-start | bytes 2752520 | tf_op jit(solution)/shard_map/ppermute | solution.py:38
  71.1 38.9 %collective-permute-start.2 = (bf16[64,7168]{1,0:T(8,128)(2,1)}, bf16[64,7168]{1,0:T(8,128)(2,1)}, u32[]{:S(2)}, u32[]{:S(2)}) collective-permute-start(bf16[64,7168]{1,0:T(8,128)(2,1)} %collective-permute-done.refs_1_), channel_id=1, source_target_pairs={{0,32},{1,33},{128,160},{129,161},{2,34},{3,35},{130,162},{131,163... | collective-permute-start | bytes 2752520 | tf_op jit(solution)/shard_map/ppermute | solution.py:38
  72.3 38.6 %collective-permute-start.5 = (bf16[64,7168]{1,0:T(8,128)(2,1)}, bf16[64,7168]{1,0:T(8,128)(2,1)}, u32[]{:S(2)}, u32[]{:S(2)}) collective-permute-start(bf16[64,7168]{1,0:T(8,128)(2,1)} %collective-permute-done.4.refs_6_), channel_id=1, source_target_pairs={{0,96},{1,97},{128,224},{129,225},{2,98},{3,99},{130,226},{131,227... | collective-permute-start | bytes 2752520 | tf_op jit(solution)/shard_map/ppermute | solution.py:38
  124.5 1.9 copy-start.1
  124.6 1.8 collective-permute-start.6
  126.4 0.7 copy-start.3
  135.5 1.0 copy-start.2
  135.5 1.1 copy-start.4
  185.0 29.1 %copy-start.8 = (s32[16]{0:T(128)S(1)}, s32[16]{0:T(128)}, u32[]{:S(2)}) copy-start(s32[16]{0:T(128)} %param.19) | copy-start | bytes 196
  209.7 26.3 %all-to-all-start.1 = ((bf16[8,16,3072]{2,1,0:T(8,128)(2,1)}), bf16[8,16,3072]{2,1,0:T(8,128)(2,1)S(1)}, u32[]{:S(2)}, u32[]{:S(2)}) async-start(bf16[8,16,3072]{2,1,0:T(8,128)(2,1)} %bitcast.10), calls=%async_computation.2 | async-start | bytes 1572864 | tf_op jit(solution)/shard_map/all_to_all | solution.py:42
  214.1 3.7 %copy-start.6 = (bf16[16,64,256]{2,1,0:T(8,128)(2,1)S(1)}, bf16[16,64,256]{2,1,0:T(8,128)(2,1)}, u32[]{:S(2)}) copy-start(bf16[16,64,256]{2,1,0:T(8,128)(2,1)} %param.18) | copy-start | bytes 1572868
  214.1 3.7 %copy-start.7 = (bf16[16,64,64]{2,1,0:T(8,128)(2,1)S(1)}, bf16[16,64,64]{2,1,0:T(8,128)(2,1)}, u32[]{:S(2)}) copy-start(bf16[16,64,64]{2,1,0:T(8,128)(2,1)} %param.16) | copy-start | bytes 393220
Sparse Core Ops, SparseCore 0:
  11.6 98.2 all-gather.1
  135.6 60.2 reduce-scatter.1
where the time goes:
time: 244 us
  waiting for transfers between devices  103 us (42%)
  blocking collectives  57.1 us (23%)
  Pallas kernels  27.1 us (11%)
  starting transfers between devices  15.9 us (7%)
  between operations  14.2 us (6%)
  matrix products  10.4 us (4%)
  local copies, waits for them, and re-layouts  9.3 us (4%)
  other arithmetic  6.86 us (3%)
    ppermute x12, waiting for transfers between devices, shift(): return lax.ppermute(value, AXES, pairs)  83.1 us
    all_to_all x2, blocking collectives, exchange_sum(): got = lax.all_to_all(blocks, axis, split_axis=0, concat_axis=0, tiled=True)  57.1 us
    pallas_call x1, Pallas kernels, hidden_units(): pl.pallas_call(hidden_kernel, out_shape=jax.ShapeDtypeStruct((NC, count /...  13.6 us
    pallas_call x2, Pallas kernels, project(): pl.pallas_call(functools.partial(down_kernel, turn), out_shape=jax.ShapeD...  13.5 us
    all_to_all x1, waiting for transfers between devices, exchange_sum(): got = lax.all_to_all(blocks, axis, split_axis=0, concat_axis=0, tiled=True)  12.4 us
    ppermute x12, starting transfers between devices, shift(): return lax.ppermute(value, AXES, pairs)  11.5 us
    unnamed x24, local copies, waits for them, and re-layouts  8.31 us
    reduce_scatter x1, waiting for transfers between devices, on_device(): lax.psum_scatter(out_b, ('zh', 'zl'), scatter_dimension=0, tiled=True)  7.34 us
  transfers between devices with their start and end apart: 15, of which 10 were waited for; matrix products, arithmetic and copies ran while one was open for 8% of the time, Pallas kernels for 8%

commit v1 on v0

--- a/solution.py
+++ b/solution.py
@@ -36,6 +36,13 @@
                         )
                     )
     return lax.ppermute(value, AXES, pairs)
+
+
+def scatter_y(blocks):
+    total = blocks[0].astype(jnp.float32)
+    for d in range(1, NY):
+        total = total + shift(blocks[d], y=d).astype(jnp.float32)
+    return total.astype(jnp.bfloat16)
 
 
 def exchange_sum(blocks, axis):
@@ -141,35 +148,46 @@
     )(jnp.reshape(expert, (1,)).astype(jnp.int32), everyone, *pieces)
 
 
-def down_kernel(turn, place_ref, mine_ref, recv_ref, own_ref, twin_ref, out_ref, acts):
+def down_kernel(turn, place_ref, mine_ref, recv_ref, own_ref, twin_ref, *refs):
+    outs, acts = refs[:-1], refs[-1]
     gates = own_ref.shape[0]
+    count = mine_ref.shape[1]
+    rows = count // (NY * NZ)
 
     @pl.when(pl.program_id(0) == 0)
     def _():
-        if not turn:
-            acts[:, :gates] = mine_ref[0]
-            acts[:, gates:] = recv_ref[...]
+        if turn:
+            pairs = [
+                (pl.ds((y * NZ + z) * rows, rows), pl.ds((z * NY + y) * rows, rows))
+                for z in range(NZ)
+                for y in range(NY)
+            ]
         else:
-            rows = mine_ref.shape[1] // (NY * NZ)
-            for z in range(NZ):
-                for y in range(NY):
-                    source = pl.ds((y * NZ + z) * rows, rows)
-                    target = pl.ds((z * NY + y) * rows, rows)
-                    acts[target, :gates] = mine_ref[0, source, :]
-                    acts[target, gates:] = recv_ref[source, :]
+            group = count // NY
+            pairs = []
+            for d in range(NY):
+                first = lax.rem(place_ref[1] + d, NY) * group
+                pairs.append((pl.ds(pl.multiple_of(first, group), group), pl.ds(d * group, group)))
+        for source, target in pairs:
+            acts[target, :gates] = mine_ref[0, source, :]
+            acts[target, gates:] = recv_ref[source, :]
 
     out = jnp.dot(acts[:, :gates], own_ref[...], preferred_element_type=jnp.float32)
     out = out + jnp.dot(acts[:, gates:], twin_ref[...], preferred_element_type=jnp.float32)
-    out_ref[...] = out.astype(jnp.bfloat16)
+    out = out.astype(jnp.bfloat16)
+    part = count // len(outs)
+    for i, out_ref in enumerate(outs):
+        out_ref[...] = out[i * part : (i + 1) * part]
 
 
 def project(acts, recv, own, twin, place, first, span, turn):
     _, count, gates = acts.shape
     block = 512
     skip = first // block
+    number = 1 if turn else NY
     return pl.pallas_call(
         functools.partial(down_kernel, turn),
-        out_shape=jax.ShapeDtypeStruct((count, span), jnp.bfloat16),
+        out_shape=[jax.ShapeDtypeStruct((count // number, span), jnp.bfloat16)] * number,
         grid_spec=pltpu.PrefetchScalarGridSpec(
             num_scalar_prefetch=1,
             grid=(span // block,),
@@ -179,10 +197,10 @@
                 pl.BlockSpec((gates, block), lambda i, p: (0, i + skip)),
                 pl.BlockSpec((gates, block), lambda i, p: (0, i + skip)),
             ],
-            out_specs=pl.BlockSpec((count, block), lambda i, p: (0, i)),
+            out_specs=[pl.BlockSpec((count // number, block), lambda i, p: (0, i))] * number,
             scratch_shapes=[pltpu.VMEM((count, 2 * gates), jnp.bfloat16)],
         ),
-        compiler_params=pltpu.CompilerParams(vmem_limit_bytes=(56 if turn else 16) << 20),
+        compiler_params=pltpu.CompilerParams(vmem_limit_bytes=50 << 20),
         cost_estimate=pl.CostEstimate(
             flops=4 * count * gates * span,
             bytes_accessed=2 * (2 * gates * span + count * span + 2 * count * gates),
@@ -209,7 +227,8 @@
     experts = router.shape[1]
     cut = width // 7 * 3
     core = lax.axis_index("c")
-    place = jnp.reshape(core, (1,)).astype(jnp.int32)
+    place_y = lax.axis_index("y")
+    place = jnp.stack([core, place_y]).astype(jnp.int32)
     expert = lax.axis_index("y") * (NZ // 2) + lax.axis_index("zh")
 
     mixing = mixing_table(hidden, expert_ids, router)
@@ -241,13 +260,15 @@
     acts = hidden_units(everyone, pieces, expert)
     recv = shift(lax.dynamic_index_in_dim(acts, 1 - core, axis=0, keepdims=False), c=1)
 
-    out_b = project(acts, recv, down, twin, place, cut, width - cut, True)
+    (out_b,) = project(acts, recv, down, twin, place, cut, width - cut, True)
     out_b = lax.psum_scatter(out_b, ("zh", "zl"), scatter_dimension=0, tiled=True)
     out_a = project(acts, recv, down, twin, place, 0, cut, False)
-    out_a = exchange_sum(out_a.reshape(NY, NZ * rows, cut), "y")
-    out_a, out_b = lax.optimization_barrier((out_a, out_b))
+    out_a = scatter_y(out_a)
     out_a = exchange_sum(out_a.reshape(NZ, rows, cut), ("zh", "zl"))
-    out_b = exchange_sum(out_b.reshape(NY, rows, width - cut), "y")
+    out_b = out_b.reshape(NY, rows, width - cut)
+    out_b = scatter_y(
+        [lax.dynamic_index_in_dim(out_b, (place_y + d) % NY, keepdims=False) for d in range(NY)]
+    )
     moe_out = jnp.concatenate([out_a, out_b], axis=1)
 
     return (moe_out, attn_latent)

time: 244 us -> 225 us (0.922)
  blocking collectives: 57.1 us -> 0 us
  waiting for transfers between devices: 103 us -> 122 us
  starting transfers between devices: 15.9 us -> 33.2 us
    all_to_all x2 -> x0, blocking collectives: 57.1 us -> none  [exchange_sum(): got = lax.all_to_all(blocks, axis, split_axis=0, concat_axis=0, tiled=True)]
    ppermute x12 -> x18, waiting for transfers between devices: 83.1 us -> 115 us  [shift(): return lax.ppermute(value, AXES, pairs)]
    ppermute x12 -> x18, starting transfers between devices: 11.5 us -> 24.7 us  [shift(): return lax.ppermute(value, AXES, pairs)]
    all_to_all x1, waiting for transfers between devices: 12.4 us -> 4.91 us  [exchange_sum(): got = lax.all_to_all(blocks, axis, split_axis=0, concat_axis=0, tiled=True)]
    reduce_scatter x1, waiting for transfers between devices: 7.34 us -> 2.03 us  [on_device(): lax.psum_scatter(out_b, ('zh', 'zl'), scatter_dimension=0, tiled=True)]
    all_to_all x1, starting transfers between devices: 4.37 us -> 8.35 us  [exchange_sum(): got = lax.all_to_all(blocks, axis, split_axis=0, concat_axis=0, tiled=True)]
    reduce_sum x3 -> x1, other arithmetic: 3.78 us -> 0.11 us  [exchange_sum(): return jnp.sum(got.astype(jnp.float32), axis=0).astype(jnp.bfloat16)]
    unnamed x24 -> x18, local copies, waits for them, and re-layouts: 8.31 us -> 7.59 us
  transfers between devices with their start and end apart: 15 -> 21, of which waited for: 10 -> 12; matrix products, arithmetic and copies ran while one was open for 8% -> 8% of each run, Pallas kernels for 8% -> 9%
where the time goes in v1:
time: 225 us; the launch traced here: 222 us
  waiting for transfers between devices  122 us (54%)
  starting transfers between devices  33.2 us (15%)
  Pallas kernels  28.3 us (13%)
  between operations  14.2 us (6%)
  matrix products  9.75 us (4%)
  local copies, waits for them, and re-layouts  9.67 us (4%)
  other arithmetic  5.68 us (3%)
    ppermute x18, waiting for transfers between devices, shift(): return lax.ppermute(value, AXES, pairs)  115 us
    ppermute x18, starting transfers between devices, shift(): return lax.ppermute(value, AXES, pairs)  24.7 us
    pallas_call x2, Pallas kernels, project(): pl.pallas_call(functools.partial(down_kernel, turn), out_shape=[jax.Shape...  14.7 us
    pallas_call x1, Pallas kernels, hidden_units(): pl.pallas_call(hidden_kernel, out_shape=jax.ShapeDtypeStruct((NC, count /...  13.6 us
    all_to_all x1, starting transfers between devices, exchange_sum(): got = lax.all_to_all(blocks, axis, split_axis=0, concat_axis=0, tiled=True)  8.35 us
    unnamed x18, local copies, waits for them, and re-layouts  7.59 us
    dot_general x1, matrix products, attend(): jnp.einsum('rhl,rlc->rhc', attn_probs, cache_latent, preferred_element_ty...  5.73 us
    all_to_all x1, waiting for transfers between devices, exchange_sum(): got = lax.all_to_all(blocks, axis, split_axis=0, concat_axis=0, tiled=True)  4.91 us
  transfers between devices with their start and end apart: 21, of which 12 were waited for; matrix products, arithmetic and copies ran while one was open for 8% of the time, Pallas kernels for 9%

profile of v1, /device:TPU:2, one launch (start us, length us, event | category | flops | bytes accessed | tf_op | source)
XLA Modules:
  0.0 222.4 jit_solution(8722475000493256479)
XLA Ops:
  8.2 1.4 fusion.21
  9.8 1.7 pad_maximum_fusion
  11.5 1.6 collective-permute-start.7
  14.0 1.8 copy.17
  16.8 17.1 %collective-permute-done.7 = bf16[64,7168]{1,0:T(8,128)(2,1)S(1)} collective-permute-done((bf16[64,7168]{1,0:T(8,128)(2,1)}, bf16[64,7168]{1,0:T(8,128)(2,1)S(1)}, u32[]{:S(2)}, u32[]{:S(2)}) %collective-permute-start.7) | collective-permute-done | bytes 917536 | tf_op jit(solution)/shard_map/ppermute | solution.py:38
  33.9 1.6 collective-permute-start.9
  38.2 7.0 %collective-permute-done.9 = bf16[32,7168]{1,0:T(8,128)(2,1)S(1)} collective-permute-done((bf16[32,7168]{1,0:T(8,128)(2,1)S(1)}, bf16[32,7168]{1,0:T(8,128)(2,1)S(1)}, u32[]{:S(2)}, u32[]{:S(2)}) %collective-permute-start.9) | collective-permute-done | bytes 458784 | tf_op jit(solution)/shard_map/ppermute | solution.py:38
  47.8 1.3 collective-permute-start
  49.9 2.3 %collective-permute-start.1 = (bf16[64,7168]{1,0:T(8,128)(2,1)S(1)}, bf16[64,7168]{1,0:T(8,128)(2,1)}, u32[]{:S(2)}, u32[]{:S(2)}) collective-permute-start(bf16[64,7168]{1,0:T(8,128)(2,1)S(1)} %get-tuple-element.11.refs_0_), channel_id=1, source_target_pairs={{0,96},{1,97},{128,224},{129,225},{2,98},{3,99},{130,226},{131,227... | collective-permute-start | bytes 2752520 | tf_op jit(solution)/shard_map/ppermute | solution.py:38
  52.1 18.9 %collective-permute-done.refs_1_ = bf16[64,7168]{1,0:T(8,128)(2,1)} collective-permute-done((bf16[64,7168]{1,0:T(8,128)(2,1)S(1)}, bf16[64,7168]{1,0:T(8,128)(2,1)}, u32[]{:S(2)}, u32[]{:S(2)}) %collective-permute-start) | collective-permute-done | bytes 917536 | tf_op jit(solution)/shard_map/ppermute | solution.py:38
  71.1 1.2 collective-permute-start.2
  73.4 18.6 %collective-permute-done.1.refs_2_ = bf16[64,7168]{1,0:T(8,128)(2,1)} collective-permute-done((bf16[64,7168]{1,0:T(8,128)(2,1)S(1)}, bf16[64,7168]{1,0:T(8,128)(2,1)}, u32[]{:S(2)}, u32[]{:S(2)}) %collective-permute-start.1) | collective-permute-done | bytes 917536 | tf_op jit(solution)/shard_map/ppermute | solution.py:38
  92.0 18.0 %collective-permute-done.2.refs_3_ = bf16[64,7168]{1,0:T(8,128)(2,1)} collective-permute-done((bf16[64,7168]{1,0:T(8,128)(2,1)}, bf16[64,7168]{1,0:T(8,128)(2,1)}, u32[]{:S(2)}, u32[]{:S(2)}) %collective-permute-start.2) | collective-permute-done | bytes 917536 | tf_op jit(solution)/shard_map/ppermute | solution.py:38
  111.0 13.6 %hidden_units.1.mine_ref = bf16[2,512,256]{2,1,0:T(8,128)(2,1)S(1)} custom-call(s32[1]{0:T(128)} %bitcast.2.expert_ref, bf16[1024,7296]{1,0:T(8,128)(2,1)} %all-gather.2.cloned.1.call-done.x_ref, bf16[64,7168]{1,0:T(8,128)(2,1)S(1)} %get-tuple-element.11.refs_0_, bf16[64,7168]{1,0:T(8,128)(2,1)} %collective-permute-done.refs_1_, ...), custom_call_target="tpu_custom_call" | custom-call | flops 7516192768 | bytes 22282240 | tf_op jit(solution)/shard_map/hidden_units/pallas_call | solution.py:127
  124.9 1.4 collective-permute-done.6.recv_ref
  126.4 8.7 %project.3 = bf16[512,4096]{1,0:T(8,128)(2,1)} custom-call(s32[2]{0:T(128)S(1)} %pad_add_fusion.place_ref, bf16[2,512,256]{2,1,0:T(8,128)(2,1)S(1)} %hidden_units.1.mine_ref, bf16[512,256]{1,0:T(8,128)(2,1)S(1)} %collective-permute-done.6.recv_ref, bf16[256,7168]{1,0:T(8,128)(2,1)} %constant_dynamic-update-slice_fusion.own_ref, ...), custom_call_target="tpu_custom_call" | custom-call | flops 2147483648 | bytes 8912896 | tf_op jit(solution)/shard_map/project/pallas_call | solution.py:188
  135.1 6.0 %project.2 = (bf16[128,3072]{1,0:T(8,128)(2,1)S(1)}, bf16[128,3072]{1,0:T(8,128)(2,1)S(1)}, bf16[128,3072]{1,0:T(8,128)(2,1)S(1)}, bf16[128,3072]{1,0:T(8,128)(2,1)S(1)}) custom-call(s32[2]{0:T(128)S(1)} %pad_add_fusion.place_ref, bf16[2,512,256]{2,1,0:T(8,128)(2,1)S(1)} %hidden_units.1.mine_ref, bf16[512,256]{1,0:T(8,128)(2,1)S(1)} %collective-permute-done.6.recv_ref, ...), custom_call_target="tpu_custom_call" | custom-call | flops 1610612736 | bytes 6815744 | tf_op jit(solution)/shard_map/project/pallas_call | solution.py:188
  141.1 2.7 %collective-permute-start.12 = (bf16[128,3072]{1,0:T(8,128)(2,1)S(1)}, bf16[128,3072]{1,0:T(8,128)(2,1)S(1)}, u32[]{:S(2)}, u32[]{:S(2)}) collective-permute-start(bf16[128,3072]{1,0:T(8,128)(2,1)S(1)} %get-tuple-element.7), channel_id=1, source_target_pairs={{0,8},{1,9},{128,136},{129,137},{2,10},{3,11},{130,138},{131,139},... | collective-permute-start | bytes 2359304 | tf_op jit(solution)/shard_map/ppermute | solution.py:38
  143.8 3.0 %collective-permute-start.13 = (bf16[128,3072]{1,0:T(8,128)(2,1)S(1)}, bf16[128,3072]{1,0:T(8,128)(2,1)S(1)}, u32[]{:S(2)}, u32[]{:S(2)}) collective-permute-start(bf16[128,3072]{1,0:T(8,128)(2,1)S(1)} %get-tuple-element.8), channel_id=1, source_target_pairs={{0,16},{1,17},{128,144},{129,145},{2,18},{3,19},{130,146},{131,147... | collective-permute-start | bytes 2359304 | tf_op jit(solution)/shard_map/ppermute | solution.py:38
  146.8 1.2 collective-permute-start.14
  148.1 1.4 fusion.23
  149.5 13.7 %collective-permute-done.12 = bf16[128,3072]{1,0:T(8,128)(2,1)S(1)} collective-permute-done((bf16[128,3072]{1,0:T(8,128)(2,1)S(1)}, bf16[128,3072]{1,0:T(8,128)(2,1)S(1)}, u32[]{:S(2)}, u32[]{:S(2)}) %collective-permute-start.12) | collective-permute-done | bytes 786464 | tf_op jit(solution)/shard_map/ppermute | solution.py:38
  163.2 18.0 %collective-permute-done.13 = bf16[128,3072]{1,0:T(8,128)(2,1)S(1)} collective-permute-done((bf16[128,3072]{1,0:T(8,128)(2,1)S(1)}, bf16[128,3072]{1,0:T(8,128)(2,1)S(1)}, u32[]{:S(2)}, u32[]{:S(2)}) %collective-permute-start.13) | collective-permute-done | bytes 786464 | tf_op jit(solution)/shard_map/ppermute | solution.py:38
  181.2 1.4 add_convert_fusion
  182.7 8.4 %all-to-all-start = ((bf16[8,16,3072]{2,1,0:T(8,128)(2,1)}), bf16[8,16,3072]{2,1,0:T(8,128)(2,1)S(1)}, u32[]{:S(2)}, u32[]{:S(2)}) async-start(bf16[8,16,3072]{2,1,0:T(8,128)(2,1)} %bitcast.37), calls=%async_computation | async-start | bytes 1572864 | tf_op jit(solution)/shard_map/all_to_all | solution.py:49
  191.1 1.3 fusion.5
  193.7 2.0 reduce-scatter.2.cloned.1.call-done
  196.8 1.6 collective-permute-start.15
  198.5 2.5 %collective-permute-start.16 = (bf16[16,4096]{1,0:T(8,128)(2,1)S(1)}, bf16[16,4096]{1,0:T(8,128)(2,1)S(1)}, u32[]{:S(2)}, u32[]{:S(2)}) collective-permute-start(bf16[16,4096]{1,0:T(8,128)(2,1)S(1)} %get-tuple-element.14), channel_id=1, source_target_pairs={{0,16},{1,17},{128,144},{129,145},{2,18},{3,19},{130,146},{131,147... | collective-permute-start | bytes 393224 | tf_op jit(solution)/shard_map/ppermute | solution.py:38
  201.0 2.1 collective-permute-start.17
  203.1 5.7 %convolution_convert_fusion = bf16[16,64,512]{2,1,0:T(8,128)(2,1)} fusion(bf16[16,256,512]{2,1,0:T(8,128)(2,1)} %param.17, f32[16,64]{1,0:T(8,128)S(1)} %fusion.22, f32[16,64,256]{2,1,0:T(8,128)} %copy-done.2, pred[16,256]{1,0:T(8,128)(4,1)S(1)} %iota_compare_fusion.1), kind=kOutput, calls=%fused_computation.4 | convolution fusion | flops 270009600 | bytes 6299648 | tf_op jit(solution)/shard_map/rhl,rlc->rhc/dot_general | solution.py:70
  208.8 4.9 %all-to-all-done = bf16[8,16,3072]{2,1,0:T(8,128)(2,1)S(1)} async-done(((bf16[8,16,3072]{2,1,0:T(8,128)(2,1)}), bf16[8,16,3072]{2,1,0:T(8,128)(2,1)S(1)}, u32[]{:S(2)}, u32[]{:S(2)}) %all-to-all-start) | async-done | bytes 786464 | tf_op jit(solution)/shard_map/all_to_all | solution.py:49
  (54 shorter events, 15.9 us)
Async XLA Ops:
  7.2 140.9 %copy-start = (bf16[16,64,512]{2,1,0:T(8,128)(2,1)S(1)}, bf16[16,64,512]{2,1,0:T(8,128)(2,1)}, u32[]{:S(2)}) copy-start(bf16[16,64,512]{2,1,0:T(8,128)(2,1)} %param.15) | copy-start | bytes 3145732
  7.2 8.6 %copy-start.3 = (bf16[1,64,7168]{2,1,0:T(8,128)(2,1)S(1)}, bf16[1,64,7168]{2,1,0:T(8,128)(2,1)}, u32[]{:S(2)}) copy-start(bf16[1,64,7168]{2,1,0:T(8,128)(2,1)} %param.14) | copy-start | bytes 2752516
  7.2 103.8 %all-gather.2.cloned.1.call-start = ((), (), s32[]{:S(2)}) async-start(), calls=%async_computation.2 | async-start | bytes 15175680 | tf_op jit(solution)/shard_map/all_gather | solution.py:239
  11.5 184.3 %reduce-scatter.2.cloned.1.call-start = ((), (), s32[]{:S(2)}) async-start(), calls=%async_computation.3 | async-start | bytes 4718592 | tf_op jit(solution)/shard_map/reduce_scatter | solution.py:264
  11.5 22.4 %collective-permute-start.7 = (bf16[64,7168]{1,0:T(8,128)(2,1)}, bf16[64,7168]{1,0:T(8,128)(2,1)S(1)}, u32[]{:S(2)}, u32[]{:S(2)}) collective-permute-start(bf16[64,7168]{1,0:T(8,128)(2,1)} %bitcast.38), channel_id=1, source_target_pairs={{0,32},{1,33},{128,160},{129,161},{2,34},{3,35},{130,162},{131,163... | collective-permute-start | bytes 2752520 | tf_op jit(solution)/shard_map/ppermute | solution.py:38
  13.1 22.4 %collective-permute-start.8 = (bf16[64,7168]{1,0:T(8,128)(2,1)}, bf16[64,7168]{1,0:T(8,128)(2,1)S(1)}, u32[]{:S(2)}, u32[]{:S(2)}) collective-permute-start(bf16[64,7168]{1,0:T(8,128)(2,1)} %bitcast.39), channel_id=1, source_target_pairs={{0,96},{1,97},{128,224},{129,225},{2,98},{3,99},{130,226},{131,227... | collective-permute-start | bytes 2752520 | tf_op jit(solution)/shard_map/ppermute | solution.py:38
  33.9 11.3 %collective-permute-start.9 = (bf16[32,7168]{1,0:T(8,128)(2,1)S(1)}, bf16[32,7168]{1,0:T(8,128)(2,1)S(1)}, u32[]{:S(2)}, u32[]{:S(2)}) collective-permute-start(bf16[32,7168]{1,0:T(8,128)(2,1)S(1)} %slice.18), channel_id=1, source_target_pairs={{0,32},{1,33},{128,160},{129,161},{2,34},{3,35},{130,162},{131,163... | collective-permute-start | bytes 1376264 | tf_op jit(solution)/shard_map/ppermute | solution.py:38
  35.5 11.3 %collective-permute-start.10 = (bf16[32,7168]{1,0:T(8,128)(2,1)S(1)}, bf16[32,7168]{1,0:T(8,128)(2,1)S(1)}, u32[]{:S(2)}, u32[]{:S(2)}) collective-permute-start(bf16[32,7168]{1,0:T(8,128)(2,1)S(1)} %slice.19), channel_id=1, source_target_pairs={{0,96},{1,97},{128,224},{129,225},{2,98},{3,99},{130,226},{131,227... | collective-permute-start | bytes 1376264 | tf_op jit(solution)/shard_map/ppermute | solution.py:38
  47.6 77.3 %collective-permute-start.11 = (bf16[256,7168]{1,0:T(8,128)(2,1)}, bf16[256,7168]{1,0:T(8,128)(2,1)}, u32[]{:S(2)}, u32[]{:S(2)}) collective-permute-start(bf16[256,7168]{1,0:T(8,128)(2,1)} %constant_dynamic-update-slice_fusion.own_ref), channel_id=1, source_target_pairs={{0,1},{1,0},{128,129},{129,128},{2,3},{3,2},{130,131},{131,130},{4... | collective-permute-start | bytes 11010056 | tf_op jit(solution)/shard_map/ppermute | solution.py:38
  47.8 23.3 %collective-permute-start = (bf16[64,7168]{1,0:T(8,128)(2,1)S(1)}, bf16[64,7168]{1,0:T(8,128)(2,1)}, u32[]{:S(2)}, u32[]{:S(2)}) collective-permute-start(bf16[64,7168]{1,0:T(8,128)(2,1)S(1)} %get-tuple-element.11.refs_0_), channel_id=1, source_target_pairs={{0,32},{1,33},{128,160},{129,161},{2,34},{3,35},{130,162},{131,163... | collective-permute-start | bytes 2752520 | tf_op jit(solution)/shard_map/ppermute | solution.py:38
  49.0 23.3 %collective-permute-start.4 = (bf16[64,7168]{1,0:T(8,128)(2,1)S(1)}, bf16[64,7168]{1,0:T(8,128)(2,1)}, u32[]{:S(2)}, u32[]{:S(2)}) collective-permute-start(bf16[64,7168]{1,0:T(8,128)(2,1)S(1)} %get-tuple-element.10.refs_4_), channel_id=1, source_target_pairs={{0,96},{1,97},{128,224},{129,225},{2,98},{3,99},{130,226},{131,227... | collective-permute-start | bytes 2752520 | tf_op jit(solution)/shard_map/ppermute | solution.py:38
  49.9 42.1 %collective-permute-start.1 = (bf16[64,7168]{1,0:T(8,128)(2,1)S(1)}, bf16[64,7168]{1,0:T(8,128)(2,1)}, u32[]{:S(2)}, u32[]{:S(2)}) collective-permute-start(bf16[64,7168]{1,0:T(8,128)(2,1)S(1)} %get-tuple-element.11.refs_0_), channel_id=1, source_target_pairs={{0,96},{1,97},{128,224},{129,225},{2,98},{3,99},{130,226},{131,227... | collective-permute-start | bytes 2752520 | tf_op jit(solution)/shard_map/ppermute | solution.py:38
  52.1 39.8 %collective-permute-start.3 = (bf16[64,7168]{1,0:T(8,128)(2,1)S(1)}, bf16[64,7168]{1,0:T(8,128)(2,1)}, u32[]{:S(2)}, u32[]{:S(2)}) collective-permute-start(bf16[64,7168]{1,0:T(8,128)(2,1)S(1)} %get-tuple-element.10.refs_4_), channel_id=1, source_target_pairs={{0,32},{1,33},{128,160},{129,161},{2,34},{3,35},{130,162},{131,163... | collective-permute-start | bytes 2752520 | tf_op jit(solution)/shard_map/ppermute | solution.py:38
  71.1 38.9 %collective-permute-start.2 = (bf16[64,7168]{1,0:T(8,128)(2,1)}, bf16[64,7168]{1,0:T(8,128)(2,1)}, u32[]{:S(2)}, u32[]{:S(2)}) collective-permute-start(bf16[64,7168]{1,0:T(8,128)(2,1)} %collective-permute-done.refs_1_), channel_id=1, source_target_pairs={{0,32},{1,33},{128,160},{129,161},{2,34},{3,35},{130,162},{131,163... | collective-permute-start | bytes 2752520 | tf_op jit(solution)/shard_map/ppermute | solution.py:38
  72.3 38.6 %collective-permute-start.5 = (bf16[64,7168]{1,0:T(8,128)(2,1)}, bf16[64,7168]{1,0:T(8,128)(2,1)}, u32[]{:S(2)}, u32[]{:S(2)}) collective-permute-start(bf16[64,7168]{1,0:T(8,128)(2,1)} %collective-permute-done.4.refs_6_), channel_id=1, source_target_pairs={{0,96},{1,97},{128,224},{129,225},{2,98},{3,99},{130,226},{131,227... | collective-permute-start | bytes 2752520 | tf_op jit(solution)/shard_map/ppermute | solution.py:38
  124.6 1.8 collective-permute-start.6
  135.1 13.0 %copy-start.1 = (bf16[16,256,512]{2,1,0:T(8,128)(2,1)S(1)}, bf16[16,256,512]{2,1,0:T(8,128)(2,1)}, u32[]{:S(2)}) copy-start(bf16[16,256,512]{2,1,0:T(8,128)(2,1)} %param.17) | copy-start | bytes 12582916
  141.1 22.1 %collective-permute-start.12 = (bf16[128,3072]{1,0:T(8,128)(2,1)S(1)}, bf16[128,3072]{1,0:T(8,128)(2,1)S(1)}, u32[]{:S(2)}, u32[]{:S(2)}) collective-permute-start(bf16[128,3072]{1,0:T(8,128)(2,1)S(1)} %get-tuple-element.7), channel_id=1, source_target_pairs={{0,8},{1,9},{128,136},{129,137},{2,10},{3,11},{130,138},{131,139},... | collective-permute-start | bytes 2359304 | tf_op jit(solution)/shard_map/ppermute | solution.py:38
  143.8 37.4 %collective-permute-start.13 = (bf16[128,3072]{1,0:T(8,128)(2,1)S(1)}, bf16[128,3072]{1,0:T(8,128)(2,1)S(1)}, u32[]{:S(2)}, u32[]{:S(2)}) collective-permute-start(bf16[128,3072]{1,0:T(8,128)(2,1)S(1)} %get-tuple-element.8), channel_id=1, source_target_pairs={{0,16},{1,17},{128,144},{129,145},{2,18},{3,19},{130,146},{131,147... | collective-permute-start | bytes 2359304 | tf_op jit(solution)/shard_map/ppermute | solution.py:38
  146.8 34.4 %collective-permute-start.14 = (bf16[128,3072]{1,0:T(8,128)(2,1)S(1)}, bf16[128,3072]{1,0:T(8,128)(2,1)S(1)}, u32[]{:S(2)}, u32[]{:S(2)}) collective-permute-start(bf16[128,3072]{1,0:T(8,128)(2,1)S(1)} %get-tuple-element.9), channel_id=1, source_target_pairs={{0,24},{1,25},{128,152},{129,153},{2,26},{3,27},{130,154},{131,155... | collective-permute-start | bytes 2359304 | tf_op jit(solution)/shard_map/ppermute | solution.py:38
  149.4 41.6 %copy-start.5 = (s32[16]{0:T(128)S(1)}, s32[16]{0:T(128)}, u32[]{:S(2)}) copy-start(s32[16]{0:T(128)} %param.19) | copy-start | bytes 196
  149.5 41.6 %copy-start.4 = (bf16[16,64,256]{2,1,0:T(8,128)(2,1)S(1)}, bf16[16,64,256]{2,1,0:T(8,128)(2,1)}, u32[]{:S(2)}) copy-start(bf16[16,64,256]{2,1,0:T(8,128)(2,1)} %param.18) | copy-start | bytes 1572868
  182.7 31.1 %all-to-all-start = ((bf16[8,16,3072]{2,1,0:T(8,128)(2,1)}), bf16[8,16,3072]{2,1,0:T(8,128)(2,1)S(1)}, u32[]{:S(2)}, u32[]{:S(2)}) async-start(bf16[8,16,3072]{2,1,0:T(8,128)(2,1)} %bitcast.37), calls=%async_computation | async-start | bytes 1572864 | tf_op jit(solution)/shard_map/all_to_all | solution.py:49
  192.4 1.0 copy-start.2
  196.8 17.0 %collective-permute-start.15 = (bf16[16,4096]{1,0:T(8,128)(2,1)S(1)}, bf16[16,4096]{1,0:T(8,128)(2,1)S(1)}, u32[]{:S(2)}, u32[]{:S(2)}) collective-permute-start(bf16[16,4096]{1,0:T(8,128)(2,1)S(1)} %get-tuple-element.12), channel_id=1, source_target_pairs={{0,8},{1,9},{128,136},{129,137},{2,10},{3,11},{130,138},{131,139},... | collective-permute-start | bytes 393224 | tf_op jit(solution)/shard_map/ppermute | solution.py:38
  198.5 15.4 %collective-permute-start.16 = (bf16[16,4096]{1,0:T(8,128)(2,1)S(1)}, bf16[16,4096]{1,0:T(8,128)(2,1)S(1)}, u32[]{:S(2)}, u32[]{:S(2)}) collective-permute-start(bf16[16,4096]{1,0:T(8,128)(2,1)S(1)} %get-tuple-element.14), channel_id=1, source_target_pairs={{0,16},{1,17},{128,144},{129,145},{2,18},{3,19},{130,146},{131,147... | collective-permute-start | bytes 393224 | tf_op jit(solution)/shard_map/ppermute | solution.py:38
  201.0 12.9 %collective-permute-start.17 = (bf16[16,4096]{1,0:T(8,128)(2,1)S(1)}, bf16[16,4096]{1,0:T(8,128)(2,1)S(1)}, u32[]{:S(2)}, u32[]{:S(2)}) collective-permute-start(bf16[16,4096]{1,0:T(8,128)(2,1)S(1)} %get-tuple-element.13), channel_id=1, source_target_pairs={{0,24},{1,25},{128,152},{129,153},{2,26},{3,27},{130,154},{131,155... | collective-permute-start | bytes 393224 | tf_op jit(solution)/shard_map/ppermute | solution.py:38
Sparse Core Ops, SparseCore 0:
  11.6 98.2 all-gather.1
  135.2 60.5 reduce-scatter.1

commit v2 on v1

--- a/solution.py
+++ b/solution.py
@@ -38,11 +38,27 @@
     return lax.ppermute(value, AXES, pairs)
 
 
+def marker(value):
+    return jnp.isnan(value[0, 0]).astype(jnp.int32)
+
+
 def scatter_y(blocks):
     total = blocks[0].astype(jnp.float32)
     for d in range(1, NY):
         total = total + shift(blocks[d], y=d).astype(jnp.float32)
     return total.astype(jnp.bfloat16)
+
+
+def add(*values):
+    return sum(v.astype(jnp.float32) for v in values).astype(jnp.bfloat16)
+
+
+def scatter_ring_y(blocks):
+    half = blocks[0].shape[1] // 2
+    up, down = shift(blocks[2][:, :half], y=1), shift(blocks[2][:, half:], y=-1)
+    up = jnp.concatenate([add(up, blocks[1][:, :half]), blocks[1][:, half:]], axis=1)
+    down = jnp.concatenate([blocks[3][:, :half], add(down, blocks[3][:, half:])], axis=1)
+    return add(blocks[0], shift(up, y=1), shift(down, y=-1))
 
 
 def exchange_sum(blocks, axis):
@@ -180,10 +196,11 @@
         out_ref[...] = out[i * part : (i + 1) * part]
 
 
-def project(acts, recv, own, twin, place, first, span, turn):
+def project(acts, recv, own, twin, place, first, span, block, turn):
     _, count, gates = acts.shape
-    block = 512
-    skip = first // block
+    window = pl.BlockSpec(
+        (pl.Element(gates), pl.Element(block)), lambda i, p: (0, pl.multiple_of(first + i * block, 128))
+    )
     number = 1 if turn else NY
     return pl.pallas_call(
         functools.partial(down_kernel, turn),
@@ -194,8 +211,8 @@
             in_specs=[
                 pl.BlockSpec((1, count, gates), lambda i, p: (p[0], 0, 0)),
                 pl.BlockSpec((count, gates), lambda i, p: (0, 0)),
-                pl.BlockSpec((gates, block), lambda i, p: (0, i + skip)),
-                pl.BlockSpec((gates, block), lambda i, p: (0, i + skip)),
+                window,
+                window,
             ],
             out_specs=[pl.BlockSpec((count // number, block), lambda i, p: (0, i))] * number,
             scratch_shapes=[pltpu.VMEM((count, 2 * gates), jnp.bfloat16)],
@@ -225,7 +242,6 @@
     rows, width = hidden.shape
     units = gate_up.shape[1]
     experts = router.shape[1]
-    cut = width // 7 * 3
     core = lax.axis_index("c")
     place_y = lax.axis_index("y")
     place = jnp.stack([core, place_y]).astype(jnp.int32)
@@ -241,7 +257,6 @@
     )
     count = everyone.shape[0]
 
-    attn_latent = attend(query_latent, query_rope, cache_latent, cache_rope, lengths)
 
     own = gate_up[0].transpose(1, 0, 2)
     gate, up = own[0], own[1]
@@ -249,10 +264,15 @@
     gate_right, up_right = shift(gate, x=-1), shift(up, x=-1)
     gate_far, up_far = shift(gate_left, x=1), shift(up_right, x=-1)
 
+    attn_latent = attend(query_latent, query_rope, cache_latent, cache_rope, lengths)
+    ready = marker(attn_latent[0])
     down = down_weight[0]
     down_left, down_right = shift(down, x=1), shift(down, x=-1)
     half = units // 2
-    far = [shift(down_left[:half], x=1), shift(down_right[half:], x=-1)]
+    far = [
+        shift(lax.dynamic_slice_in_dim(down_left, ready, half, axis=0), x=1),
+        shift(lax.dynamic_slice_in_dim(down_right, half + ready, half, axis=0), x=-1),
+    ]
     down = jnp.concatenate([down, down_left, down_right] + far, axis=0)
     twin = shift(down, c=1)
 
@@ -260,10 +280,11 @@
     acts = hidden_units(everyone, pieces, expert)
     recv = shift(lax.dynamic_index_in_dim(acts, 1 - core, axis=0, keepdims=False), c=1)
 
-    (out_b,) = project(acts, recv, down, twin, place, cut, width - cut, True)
+    cut = width // 28 * 13
+    inputs = (acts, recv, down, twin, place)
+    (out_b,) = project(*inputs, cut, width - cut, (width - cut) // 3, True)
     out_b = lax.psum_scatter(out_b, ("zh", "zl"), scatter_dimension=0, tiled=True)
-    out_a = project(acts, recv, down, twin, place, 0, cut, False)
-    out_a = scatter_y(out_a)
+    out_a = scatter_ring_y(project(*inputs, 0, cut, cut // 2, False))
     out_a = exchange_sum(out_a.reshape(NZ, rows, cut), ("zh", "zl"))
     out_b = out_b.reshape(NY, rows, width - cut)
     out_b = scatter_y(

time: 225 us -> 221 us (0.982)
  waiting for transfers between devices: 122 us -> 106 us
  starting transfers between devices: 33.2 us -> 41.8 us
  local copies, waits for them, and re-layouts: 9.67 us -> 13.5 us
  Pallas kernels: 28.3 us -> 25.3 us
    ppermute x18 -> x19, waiting for transfers between devices: 115 us -> 99.2 us  [shift(): return lax.ppermute(value, AXES, pairs)]
    ppermute x18 -> x19, starting transfers between devices: 24.7 us -> 33.3 us  [shift(): return lax.ppermute(value, AXES, pairs)]
    pallas_call x2, Pallas kernels: 14.7 us -> 11.7 us  [project(): pl.pallas_call(functools.partial(down_kernel, turn), out_shape=[jax.Shape...]
    dot_general x1, matrix products: 1.37 us -> 3.67 us  [attend(): jnp.einsum('rhc,rlc->rhl', query_latent, cache_latent, preferred_element_...]
    unnamed x18 -> x22, local copies, waits for them, and re-layouts: 7.59 us -> 8.75 us
  transfers between devices with their start and end apart: 21 -> 22, of which waited for: 12 -> 15; matrix products, arithmetic and copies ran while one was open for 8% -> 11% of each run, Pallas kernels for 9% -> 9%
where the time goes in v2:
time: 221 us; the launch traced here: 219 us
  waiting for transfers between devices  106 us (48%)
  starting transfers between devices  41.8 us (19%)
  Pallas kernels  25.3 us (11%)
  between operations  15.6 us (7%)
  local copies, waits for them, and re-layouts  13.5 us (6%)
  matrix products  11.1 us (5%)
  other arithmetic  5.79 us (3%)
    ppermute x19, waiting for transfers between devices, shift(): return lax.ppermute(value, AXES, pairs)  99.2 us
    ppermute x19, starting transfers between devices, shift(): return lax.ppermute(value, AXES, pairs)  33.3 us
    pallas_call x1, Pallas kernels, hidden_units(): pl.pallas_call(hidden_kernel, out_shape=jax.ShapeDtypeStruct((NC, count /...  13.6 us
    pallas_call x2, Pallas kernels, project(): pl.pallas_call(functools.partial(down_kernel, turn), out_shape=[jax.Shape...  11.7 us
    unnamed x22, local copies, waits for them, and re-layouts  8.75 us
    all_to_all x1, starting transfers between devices, exchange_sum(): got = lax.all_to_all(blocks, axis, split_axis=0, concat_axis=0, tiled=True)  8.36 us
    dot_general x1, matrix products, attend(): jnp.einsum('rhl,rlc->rhc', attn_probs, cache_latent, preferred_element_ty...  5.74 us
  transfers between devices with their start and end apart: 22, of which 15 were waited for; matrix products, arithmetic and copies ran while one was open for 11% of the time, Pallas kernels for 9%

profile of v2, /device:TPU:2, one launch (start us, length us, event | category | flops | bytes accessed | tf_op | source)
XLA Modules:
  0.0 219.2 jit_solution(9480926237990343917)
XLA Ops:
  8.2 1.4 fusion.22
  9.7 1.7 pad_maximum_fusion.2
  11.5 1.6 collective-permute-start.7
  13.9 3.1 %copy.17 = bf16[1,64,2,7168]{3,1,2,0:T(8,128)(2,1)} copy(bf16[1,64,2,7168]{3,2,1,0:T(2,128)(2,1)} %param.13) | data formatting | bytes 3670016 | tf_op args[3]
  17.1 3.7 %fusion.24 = f32[16,64,256]{2,1,0:T(8,128)S(1)} fusion(bf16[16,64,512]{2,1,0:T(8,128)(2,1)S(1)} %copy-done, bf16[16,256,512]{2,1,0:T(8,128)(2,1)} %param.17), kind=kOutput, calls=%fused_computation.58 | convolution fusion | flops 268435456 | bytes 6291456 | tf_op jit(solution)/shard_map/rhc,rlc->rhl/dot_general | solution.py:71
  23.5 5.7 %convolution_convert_fusion = bf16[16,64,512]{2,1,0:T(8,128)(2,1)} fusion(bf16[16,256,512]{2,1,0:T(8,128)(2,1)} %param.17, f32[16,64]{1,0:T(8,128)S(1)} %fusion.23, f32[16,64,256]{2,1,0:T(8,128)} %copy-done.2, pred[16,256]{1,0:T(8,128)(4,1)S(1)} %iota_compare_fusion.1), kind=kOutput, calls=%fused_computation.4 | convolution fusion | flops 270009600 | bytes 6299648 | tf_op jit(solution)/shard_map/rhl,rlc->rhc/dot_general | solution.py:86
  31.9 2.0 collective-permute-done.7
  34.0 1.6 collective-permute-start.9
  38.2 7.0 %collective-permute-done.9 = bf16[32,7168]{1,0:T(8,128)(2,1)S(1)} collective-permute-done((bf16[32,7168]{1,0:T(8,128)(2,1)S(1)}, bf16[32,7168]{1,0:T(8,128)(2,1)S(1)}, u32[]{:S(2)}, u32[]{:S(2)}) %collective-permute-start.9) | collective-permute-done | bytes 458784 | tf_op jit(solution)/shard_map/ppermute | solution.py:38
  47.9 1.3 collective-permute-start
  50.0 2.2 collective-permute-start.1
  52.2 19.1 %collective-permute-done.refs_1_ = bf16[64,7168]{1,0:T(8,128)(2,1)} collective-permute-done((bf16[64,7168]{1,0:T(8,128)(2,1)S(1)}, bf16[64,7168]{1,0:T(8,128)(2,1)}, u32[]{:S(2)}, u32[]{:S(2)}) %collective-permute-start) | collective-permute-done | bytes 917536 | tf_op jit(solution)/shard_map/ppermute | solution.py:38
  71.2 1.2 collective-permute-start.2
  73.4 18.7 %collective-permute-done.1.refs_2_ = bf16[64,7168]{1,0:T(8,128)(2,1)} collective-permute-done((bf16[64,7168]{1,0:T(8,128)(2,1)S(1)}, bf16[64,7168]{1,0:T(8,128)(2,1)}, u32[]{:S(2)}, u32[]{:S(2)}) %collective-permute-start.1) | collective-permute-done | bytes 917536 | tf_op jit(solution)/shard_map/ppermute | solution.py:38
  92.1 18.0 %collective-permute-done.2.refs_3_ = bf16[64,7168]{1,0:T(8,128)(2,1)} collective-permute-done((bf16[64,7168]{1,0:T(8,128)(2,1)}, bf16[64,7168]{1,0:T(8,128)(2,1)}, u32[]{:S(2)}, u32[]{:S(2)}) %collective-permute-start.2) | collective-permute-done | bytes 917536 | tf_op jit(solution)/shard_map/ppermute | solution.py:38
  111.1 13.6 %hidden_units.1.mine_ref = bf16[2,512,256]{2,1,0:T(8,128)(2,1)S(1)} custom-call(s32[1]{0:T(128)} %bitcast.2.expert_ref, bf16[1024,7296]{1,0:T(8,128)(2,1)} %all-gather.2.cloned.1.call-done.x_ref, bf16[64,7168]{1,0:T(8,128)(2,1)S(1)} %get-tuple-element.11.refs_0_, bf16[64,7168]{1,0:T(8,128)(2,1)} %collective-permute-done.refs_1_, ...), custom_call_target="tpu_custom_call" | custom-call | flops 7516192768 | bytes 22282240 | tf_op jit(solution)/shard_map/hidden_units/pallas_call | solution.py:143
  124.9 1.4 collective-permute-done.6.recv_ref
  126.3 6.5 %project.3 = bf16[512,3840]{1,0:T(8,128)(2,1)} custom-call(s32[2]{0:T(128)S(1)} %pad_add_fusion.place_ref, bf16[2,512,256]{2,1,0:T(8,128)(2,1)S(1)} %hidden_units.1.mine_ref, bf16[512,256]{1,0:T(8,128)(2,1)S(1)} %collective-permute-done.6.recv_ref, bf16[256,7168]{1,0:T(8,128)(2,1)} %constant_dynamic-update-slice_fusion.own_ref, ...), custom_call_target="tpu_custom_call" | custom-call | flops 2013265920 | bytes 8388608 | tf_op jit(solution)/shard_map/project/pallas_call | solution.py:205
  132.8 5.3 %project.2 = (bf16[128,3328]{1,0:T(8,128)(2,1)S(1)}, bf16[128,3328]{1,0:T(8,128)(2,1)S(1)}, bf16[128,3328]{1,0:T(8,128)(2,1)S(1)}, bf16[128,3328]{1,0:T(8,128)(2,1)}) custom-call(s32[2]{0:T(128)S(1)} %pad_add_fusion.place_ref, bf16[2,512,256]{2,1,0:T(8,128)(2,1)S(1)} %hidden_units.1.mine_ref, bf16[512,256]{1,0:T(8,128)(2,1)S(1)} %collective-permute-done.6.recv_ref, ...), custom_call_target="tpu_custom_call" | custom-call | flops 1744830464 | bytes 7340032 | tf_op jit(solution)/shard_map/project/pallas_call | solution.py:205
  138.2 4.2 %collective-permute-start.14 = (bf16[128,1664]{1,0:T(8,128)(2,1)S(1)}, bf16[128,1664]{1,0:T(8,128)(2,1)S(1)}, u32[]{:S(2)}, u32[]{:S(2)}) collective-permute-start(bf16[128,1664]{1,0:T(8,128)(2,1)S(1)} %get-tuple-element.13), channel_id=1, source_target_pairs={{0,24},{1,25},{128,152},{129,153},{2,26},{3,27},{130,154},{131,155... | collective-permute-start | bytes 1277960 | tf_op jit(solution)/shard_map/ppermute | solution.py:38
  143.6 8.2 %collective-permute-done.14 = bf16[128,1664]{1,0:T(8,128)(2,1)S(1)} collective-permute-done((bf16[128,1664]{1,0:T(8,128)(2,1)S(1)}, bf16[128,1664]{1,0:T(8,128)(2,1)S(1)}, u32[]{:S(2)}, u32[]{:S(2)}) %collective-permute-start.14) | collective-permute-done | bytes 426016 | tf_op jit(solution)/shard_map/ppermute | solution.py:38
  152.0 3.8 %collective-permute-start.15 = (bf16[128,3328]{1,0:T(8,128)(2,1)S(1)}, bf16[128,3328]{1,0:T(8,128)(2,1)S(1)}, u32[]{:S(2)}, u32[]{:S(2)}) collective-permute-start(bf16[128,3328]{1,0:T(8,128)(2,1)S(1)} %pad_maximum_fusion.1), channel_id=1, source_target_pairs={{0,24},{1,25},{128,152},{129,153},{2,26},{3,27},{130,154},{131,155... | collective-permute-start | bytes 2555912 | tf_op jit(solution)/shard_map/ppermute | solution.py:38
  156.6 16.8 %collective-permute-done.15 = bf16[128,3328]{1,0:T(8,128)(2,1)S(1)} collective-permute-done((bf16[128,3328]{1,0:T(8,128)(2,1)S(1)}, bf16[128,3328]{1,0:T(8,128)(2,1)S(1)}, u32[]{:S(2)}, u32[]{:S(2)}) %collective-permute-start.15) | collective-permute-done | bytes 852000 | tf_op jit(solution)/shard_map/ppermute | solution.py:38
  173.4 4.3 %collective-permute-done.13 = bf16[128,3328]{1,0:T(8,128)(2,1)S(1)} collective-permute-done((bf16[128,3328]{1,0:T(8,128)(2,1)S(1)}, bf16[128,3328]{1,0:T(8,128)(2,1)S(1)}, u32[]{:S(2)}, u32[]{:S(2)}) %collective-permute-start.13) | collective-permute-done | bytes 852000 | tf_op jit(solution)/shard_map/ppermute | solution.py:38
  177.8 1.2 add_convert_fusion
  179.0 8.4 %all-to-all-start = ((bf16[8,16,3328]{2,1,0:T(8,128)(2,1)}), bf16[8,16,3328]{2,1,0:T(8,128)(2,1)S(1)}, u32[]{:S(2)}, u32[]{:S(2)}) async-start(bf16[8,16,3328]{2,1,0:T(8,128)(2,1)} %bitcast.12), calls=%async_computation | async-start | bytes 1703936 | tf_op jit(solution)/shard_map/all_to_all | solution.py:65
  187.4 3.5 %reduce-scatter.2.cloned.1.call-done = bf16[64,3840]{1,0:T(8,128)(2,1)} async-done(((bf16[512,3840]{1,0:T(8,128)(2,1)}), bf16[64,3840]{1,0:T(8,128)(2,1)}) %reduce-scatter.2.cloned.1.call-update) | async-done | bytes 491536 | tf_op jit(solution)/shard_map/reduce_scatter | solution.py:286
  191.9 9.4 %collective-permute-start.18 = (bf16[16,3840]{1,0:T(8,128)(2,1)S(1)}, bf16[16,3840]{1,0:T(8,128)(2,1)S(1)}, u32[]{:S(2)}, u32[]{:S(2)}) collective-permute-start(bf16[16,3840]{1,0:T(8,128)(2,1)S(1)} %get-tuple-element.15), channel_id=1, source_target_pairs={{0,24},{1,25},{128,152},{129,153},{2,26},{3,27},{130,154},{131,155... | collective-permute-start | bytes 368648 | tf_op jit(solution)/shard_map/ppermute | solution.py:38
  201.3 3.3 %collective-permute-start.17 = (bf16[16,3840]{1,0:T(8,128)(2,1)S(1)}, bf16[16,3840]{1,0:T(8,128)(2,1)S(1)}, u32[]{:S(2)}, u32[]{:S(2)}) collective-permute-start(bf16[16,3840]{1,0:T(8,128)(2,1)S(1)} %get-tuple-element.16), channel_id=1, source_target_pairs={{0,16},{1,17},{128,144},{129,145},{2,18},{3,19},{130,146},{131,147... | collective-permute-start | bytes 368648 | tf_op jit(solution)/shard_map/ppermute | solution.py:38
  204.6 1.3 collective-permute-start.16
  205.9 3.5 %all-to-all-done = bf16[8,16,3328]{2,1,0:T(8,128)(2,1)S(1)} async-done(((bf16[8,16,3328]{2,1,0:T(8,128)(2,1)}), bf16[8,16,3328]{2,1,0:T(8,128)(2,1)S(1)}, u32[]{:S(2)}, u32[]{:S(2)}) %all-to-all-start) | async-done | bytes 852000 | tf_op jit(solution)/shard_map/all_to_all | solution.py:65
  209.5 1.1 collective-permute-done.16
  (69 shorter events, 19.7 us)
Async XLA Ops:
  7.2 9.9 %copy-start = (bf16[16,64,512]{2,1,0:T(8,128)(2,1)S(1)}, bf16[16,64,512]{2,1,0:T(8,128)(2,1)}, u32[]{:S(2)}) copy-start(bf16[16,64,512]{2,1,0:T(8,128)(2,1)} %param.15) | copy-start | bytes 3145732
  7.2 9.8 %copy-start.7 = (s32[16]{0:T(128)S(1)}, s32[16]{0:T(128)}, u32[]{:S(2)}) copy-start(s32[16]{0:T(128)} %param.19) | copy-start | bytes 196
  7.2 103.9 %all-gather.2.cloned.1.call-start = ((), (), s32[]{:S(2)}) async-start(), calls=%async_computation.2 | async-start | bytes 15175680 | tf_op jit(solution)/shard_map/all_gather | solution.py:255
  11.4 179.4 %reduce-scatter.2.cloned.1.call-start = ((), (), s32[]{:S(2)}) async-start(), calls=%async_computation.3 | async-start | bytes 4423680 | tf_op jit(solution)/shard_map/reduce_scatter | solution.py:286
  11.5 22.4 %collective-permute-start.7 = (bf16[64,7168]{1,0:T(8,128)(2,1)}, bf16[64,7168]{1,0:T(8,128)(2,1)S(1)}, u32[]{:S(2)}, u32[]{:S(2)}) collective-permute-start(bf16[64,7168]{1,0:T(8,128)(2,1)} %bitcast.40), channel_id=1, source_target_pairs={{0,32},{1,33},{128,160},{129,161},{2,34},{3,35},{130,162},{131,163... | collective-permute-start | bytes 2752520 | tf_op jit(solution)/shard_map/ppermute | solution.py:38
  13.0 22.5 %collective-permute-start.8 = (bf16[64,7168]{1,0:T(8,128)(2,1)}, bf16[64,7168]{1,0:T(8,128)(2,1)S(1)}, u32[]{:S(2)}, u32[]{:S(2)}) collective-permute-start(bf16[64,7168]{1,0:T(8,128)(2,1)} %bitcast.41), channel_id=1, source_target_pairs={{0,96},{1,97},{128,224},{129,225},{2,98},{3,99},{130,226},{131,227... | collective-permute-start | bytes 2752520 | tf_op jit(solution)/shard_map/ppermute | solution.py:38
  17.0 3.8 %copy-start.3 = (bf16[1,64,7168]{2,1,0:T(8,128)(2,1)S(1)}, bf16[1,64,7168]{2,1,0:T(8,128)(2,1)}, u32[]{:S(2)}) copy-start(bf16[1,64,7168]{2,1,0:T(8,128)(2,1)} %param.14) | copy-start | bytes 2752516
  17.1 4.7 %copy-start.5 = (bf16[16,64,256]{2,1,0:T(8,128)(2,1)S(1)}, bf16[16,64,256]{2,1,0:T(8,128)(2,1)}, u32[]{:S(2)}) copy-start(bf16[16,64,256]{2,1,0:T(8,128)(2,1)} %param.18) | copy-start | bytes 1572868
  17.1 4.7 %copy-start.6 = (bf16[16,64,64]{2,1,0:T(8,128)(2,1)S(1)}, bf16[16,64,64]{2,1,0:T(8,128)(2,1)}, u32[]{:S(2)}) copy-start(bf16[16,64,64]{2,1,0:T(8,128)(2,1)} %param.16) | copy-start | bytes 393220
  22.1 1.0 copy-start.2
  31.9 15.9 %copy-start.1 = (bf16[1,64,2,7168]{3,1,2,0:T(8,128)(2,1)S(1)}, bf16[1,64,2,7168]{3,1,2,0:T(8,128)(2,1)}, u32[]{:S(2)}) copy-start(bf16[1,64,2,7168]{3,1,2,0:T(8,128)(2,1)} %copy.17) | copy-start | bytes 5505028
  34.0 11.3 %collective-permute-start.9 = (bf16[32,7168]{1,0:T(8,128)(2,1)S(1)}, bf16[32,7168]{1,0:T(8,128)(2,1)S(1)}, u32[]{:S(2)}, u32[]{:S(2)}) collective-permute-start(bf16[32,7168]{1,0:T(8,128)(2,1)S(1)} %constant_dynamic-slice_fusion.1), channel_id=1, source_target_pairs={{0,32},{1,33},{128,160},{129,161},{2,34},{3,35},{130,162},{131,163... | collective-permute-start | bytes 1376264 | tf_op jit(solution)/shard_map/ppermute | solution.py:38
  35.7 11.3 %collective-permute-start.10 = (bf16[32,7168]{1,0:T(8,128)(2,1)S(1)}, bf16[32,7168]{1,0:T(8,128)(2,1)S(1)}, u32[]{:S(2)}, u32[]{:S(2)}) collective-permute-start(bf16[32,7168]{1,0:T(8,128)(2,1)S(1)} %constant_dynamic-slice_fusion), channel_id=1, source_target_pairs={{0,96},{1,97},{128,224},{129,225},{2,98},{3,99},{130,226},{131,227... | collective-permute-start | bytes 1376264 | tf_op jit(solution)/shard_map/ppermute | solution.py:38
  47.8 77.1 %collective-permute-start.11 = (bf16[256,7168]{1,0:T(8,128)(2,1)}, bf16[256,7168]{1,0:T(8,128)(2,1)}, u32[]{:S(2)}, u32[]{:S(2)}) collective-permute-start(bf16[256,7168]{1,0:T(8,128)(2,1)} %constant_dynamic-update-slice_fusion.own_ref), channel_id=1, source_target_pairs={{0,1},{1,0},{128,129},{129,128},{2,3},{3,2},{130,131},{131,130},{4... | collective-permute-start | bytes 11010056 | tf_op jit(solution)/shard_map/ppermute | solution.py:38
  47.9 23.3 %collective-permute-start = (bf16[64,7168]{1,0:T(8,128)(2,1)S(1)}, bf16[64,7168]{1,0:T(8,128)(2,1)}, u32[]{:S(2)}, u32[]{:S(2)}) collective-permute-start(bf16[64,7168]{1,0:T(8,128)(2,1)S(1)} %get-tuple-element.11.refs_0_), channel_id=1, source_target_pairs={{0,32},{1,33},{128,160},{129,161},{2,34},{3,35},{130,162},{131,163... | collective-permute-start | bytes 2752520 | tf_op jit(solution)/shard_map/ppermute | solution.py:38
  49.2 23.3 %collective-permute-start.4 = (bf16[64,7168]{1,0:T(8,128)(2,1)S(1)}, bf16[64,7168]{1,0:T(8,128)(2,1)}, u32[]{:S(2)}, u32[]{:S(2)}) collective-permute-start(bf16[64,7168]{1,0:T(8,128)(2,1)S(1)} %get-tuple-element.10.refs_4_), channel_id=1, source_target_pairs={{0,96},{1,97},{128,224},{129,225},{2,98},{3,99},{130,226},{131,227... | collective-permute-start | bytes 2752520 | tf_op jit(solution)/shard_map/ppermute | solution.py:38
  50.0 42.1 %collective-permute-start.1 = (bf16[64,7168]{1,0:T(8,128)(2,1)S(1)}, bf16[64,7168]{1,0:T(8,128)(2,1)}, u32[]{:S(2)}, u32[]{:S(2)}) collective-permute-start(bf16[64,7168]{1,0:T(8,128)(2,1)S(1)} %get-tuple-element.11.refs_0_), channel_id=1, source_target_pairs={{0,96},{1,97},{128,224},{129,225},{2,98},{3,99},{130,226},{131,227... | collective-permute-start | bytes 2752520 | tf_op jit(solution)/shard_map/ppermute | solution.py:38
  52.2 40.0 %collective-permute-start.3 = (bf16[64,7168]{1,0:T(8,128)(2,1)S(1)}, bf16[64,7168]{1,0:T(8,128)(2,1)}, u32[]{:S(2)}, u32[]{:S(2)}) collective-permute-start(bf16[64,7168]{1,0:T(8,128)(2,1)S(1)} %get-tuple-element.10.refs_4_), channel_id=1, source_target_pairs={{0,32},{1,33},{128,160},{129,161},{2,34},{3,35},{130,162},{131,163... | collective-permute-start | bytes 2752520 | tf_op jit(solution)/shard_map/ppermute | solution.py:38
  71.2 38.9 %collective-permute-start.2 = (bf16[64,7168]{1,0:T(8,128)(2,1)}, bf16[64,7168]{1,0:T(8,128)(2,1)}, u32[]{:S(2)}, u32[]{:S(2)}) collective-permute-start(bf16[64,7168]{1,0:T(8,128)(2,1)} %collective-permute-done.refs_1_), channel_id=1, source_target_pairs={{0,32},{1,33},{128,160},{129,161},{2,34},{3,35},{130,162},{131,163... | collective-permute-start | bytes 2752520 | tf_op jit(solution)/shard_map/ppermute | solution.py:38
  72.5 38.6 %collective-permute-start.5 = (bf16[64,7168]{1,0:T(8,128)(2,1)}, bf16[64,7168]{1,0:T(8,128)(2,1)}, u32[]{:S(2)}, u32[]{:S(2)}) collective-permute-start(bf16[64,7168]{1,0:T(8,128)(2,1)} %collective-permute-done.4.refs_6_), channel_id=1, source_target_pairs={{0,96},{1,97},{128,224},{129,225},{2,98},{3,99},{130,226},{131,227... | collective-permute-start | bytes 2752520 | tf_op jit(solution)/shard_map/ppermute | solution.py:38
  124.7 1.6 collective-permute-start.6
  138.1 13.7 %copy-start.4 = (bf16[128,3328]{1,0:T(8,128)(2,1)S(1)}, bf16[128,3328]{1,0:T(8,128)(2,1)}, u32[]{:S(2)}) copy-start(bf16[128,3328]{1,0:T(8,128)(2,1)} %get-tuple-element.9) | copy-start | bytes 2555908
  138.2 13.6 %collective-permute-start.14 = (bf16[128,1664]{1,0:T(8,128)(2,1)S(1)}, bf16[128,1664]{1,0:T(8,128)(2,1)S(1)}, u32[]{:S(2)}, u32[]{:S(2)}) collective-permute-start(bf16[128,1664]{1,0:T(8,128)(2,1)S(1)} %get-tuple-element.13), channel_id=1, source_target_pairs={{0,24},{1,25},{128,152},{129,153},{2,26},{3,27},{130,154},{131,155... | collective-permute-start | bytes 1277960 | tf_op jit(solution)/shard_map/ppermute | solution.py:38
  143.5 12.9 %collective-permute-start.12 = (bf16[128,1664]{1,0:T(8,128)(2,1)S(1)}, bf16[128,1664]{1,0:T(8,128)(2,1)S(1)}, u32[]{:S(2)}, u32[]{:S(2)}) collective-permute-start(bf16[128,1664]{1,0:T(8,128)(2,1)S(1)} %get-tuple-element.12), channel_id=1, source_target_pairs={{0,8},{1,9},{128,136},{129,137},{2,10},{3,11},{130,138},{131,139},... | collective-permute-start | bytes 1277960 | tf_op jit(solution)/shard_map/ppermute | solution.py:38
  152.0 21.4 %collective-permute-start.15 = (bf16[128,3328]{1,0:T(8,128)(2,1)S(1)}, bf16[128,3328]{1,0:T(8,128)(2,1)S(1)}, u32[]{:S(2)}, u32[]{:S(2)}) collective-permute-start(bf16[128,3328]{1,0:T(8,128)(2,1)S(1)} %pad_maximum_fusion.1), channel_id=1, source_target_pairs={{0,24},{1,25},{128,152},{129,153},{2,26},{3,27},{130,154},{131,155... | collective-permute-start | bytes 2555912 | tf_op jit(solution)/shard_map/ppermute | solution.py:38
  156.5 21.2 %collective-permute-start.13 = (bf16[128,3328]{1,0:T(8,128)(2,1)S(1)}, bf16[128,3328]{1,0:T(8,128)(2,1)S(1)}, u32[]{:S(2)}, u32[]{:S(2)}) collective-permute-start(bf16[128,3328]{1,0:T(8,128)(2,1)S(1)} %pad_maximum_fusion), channel_id=1, source_target_pairs={{0,8},{1,9},{128,136},{129,137},{2,10},{3,11},{130,138},{131,139},... | collective-permute-start | bytes 2555912 | tf_op jit(solution)/shard_map/ppermute | solution.py:38
  179.0 30.4 %all-to-all-start = ((bf16[8,16,3328]{2,1,0:T(8,128)(2,1)}), bf16[8,16,3328]{2,1,0:T(8,128)(2,1)S(1)}, u32[]{:S(2)}, u32[]{:S(2)}) async-start(bf16[8,16,3328]{2,1,0:T(8,128)(2,1)} %bitcast.12), calls=%async_computation | async-start | bytes 1703936 | tf_op jit(solution)/shard_map/all_to_all | solution.py:65
  191.9 17.6 %collective-permute-start.18 = (bf16[16,3840]{1,0:T(8,128)(2,1)S(1)}, bf16[16,3840]{1,0:T(8,128)(2,1)S(1)}, u32[]{:S(2)}, u32[]{:S(2)}) collective-permute-start(bf16[16,3840]{1,0:T(8,128)(2,1)S(1)} %get-tuple-element.15), channel_id=1, source_target_pairs={{0,24},{1,25},{128,152},{129,153},{2,26},{3,27},{130,154},{131,155... | collective-permute-start | bytes 368648 | tf_op jit(solution)/shard_map/ppermute | solution.py:38
  201.3 8.3 %collective-permute-start.17 = (bf16[16,3840]{1,0:T(8,128)(2,1)S(1)}, bf16[16,3840]{1,0:T(8,128)(2,1)S(1)}, u32[]{:S(2)}, u32[]{:S(2)}) collective-permute-start(bf16[16,3840]{1,0:T(8,128)(2,1)S(1)} %get-tuple-element.16), channel_id=1, source_target_pairs={{0,16},{1,17},{128,144},{129,145},{2,18},{3,19},{130,146},{131,147... | collective-permute-start | bytes 368648 | tf_op jit(solution)/shard_map/ppermute | solution.py:38
  204.6 6.1 %collective-permute-start.16 = (bf16[16,3840]{1,0:T(8,128)(2,1)S(1)}, bf16[16,3840]{1,0:T(8,128)(2,1)S(1)}, u32[]{:S(2)}, u32[]{:S(2)}) collective-permute-start(bf16[16,3840]{1,0:T(8,128)(2,1)S(1)} %get-tuple-element.14), channel_id=1, source_target_pairs={{0,8},{1,9},{128,136},{129,137},{2,10},{3,11},{130,138},{131,139},... | collective-permute-start | bytes 368648 | tf_op jit(solution)/shard_map/ppermute | solution.py:38
Sparse Core Ops, SparseCore 0:
  11.5 98.2 all-gather.1
  132.9 57.8 reduce-scatter.1

commit v3 on v2

--- a/solution.py
+++ b/solution.py
@@ -56,9 +56,13 @@
 def scatter_ring_y(blocks):
     half = blocks[0].shape[1] // 2
     up, down = shift(blocks[2][:, :half], y=1), shift(blocks[2][:, half:], y=-1)
-    up = jnp.concatenate([add(up, blocks[1][:, :half]), blocks[1][:, half:]], axis=1)
-    down = jnp.concatenate([blocks[3][:, :half], add(down, blocks[3][:, half:])], axis=1)
-    return add(blocks[0], shift(up, y=1), shift(down, y=-1))
+    free_up, free_down = shift(blocks[1][:, half:], y=1), shift(blocks[3][:, :half], y=-1)
+    up = shift(add(up, blocks[1][:, :half]), y=1)
+    down = shift(add(down, blocks[3][:, half:]), y=-1)
+    own = blocks[0]
+    return jnp.concatenate(
+        [add(own[:, :half], up, free_down), add(own[:, half:], free_up, down)], axis=1
+    )
 
 
 def exchange_sum(blocks, axis):

time: 221 us -> 219 us (level)
  waiting for transfers between devices: 106 us -> 112 us
  starting transfers between devices: 41.8 us -> 36.3 us
    reduce_scatter x1, waiting for transfers between devices: 3.48 us -> 13.4 us  [on_device(): lax.psum_scatter(out_b, ('zh', 'zl'), scatter_dimension=0, tiled=True)]
    ppermute x19 -> x21, waiting for transfers between devices: 99.2 us -> 93 us  [shift(): return lax.ppermute(value, AXES, pairs)]
    ppermute x19 -> x21, starting transfers between devices: 33.3 us -> 27.9 us  [shift(): return lax.ppermute(value, AXES, pairs)]
  transfers between devices with their start and end apart: 22 -> 24, of which waited for: 15 -> 14; matrix products, arithmetic and copies ran while one was open for 11% -> 11% of each run, Pallas kernels for 9% -> 9%
where the time goes in v3:
time: 219 us
  waiting for transfers between devices  112 us (51%)
  starting transfers between devices  36.3 us (17%)
  Pallas kernels  25.4 us (12%)
  between operations  15.5 us (7%)
  local copies, waits for them, and re-layouts  13.4 us (6%)
  matrix products  11.1 us (5%)
  other arithmetic  5.71 us (3%)
    ppermute x21, waiting for transfers between devices, shift(): return lax.ppermute(value, AXES, pairs)  93 us
    ppermute x21, starting transfers between devices, shift(): return lax.ppermute(value, AXES, pairs)  27.9 us
    pallas_call x1, Pallas kernels, hidden_units(): pl.pallas_call(hidden_kernel, out_shape=jax.ShapeDtypeStruct((NC, count /...  13.6 us
    reduce_scatter x1, waiting for transfers between devices, on_device(): lax.psum_scatter(out_b, ('zh', 'zl'), scatter_dimension=0, tiled=True)  13.4 us
    pallas_call x2, Pallas kernels, project(): pl.pallas_call(functools.partial(down_kernel, turn), out_shape=[jax.Shape...  11.8 us
    unnamed x22, local copies, waits for them, and re-layouts  8.7 us
    all_to_all x1, starting transfers between devices, exchange_sum(): got = lax.all_to_all(blocks, axis, split_axis=0, concat_axis=0, tiled=True)  8.24 us
    dot_general x1, matrix products, attend(): jnp.einsum('rhl,rlc->rhc', attn_probs, cache_latent, preferred_element_ty...  5.74 us
  transfers between devices with their start and end apart: 24, of which 14 were waited for; matrix products, arithmetic and copies ran while one was open for 11% of the time, Pallas kernels for 9%

profile of v3, /device:TPU:2, one launch (start us, length us, event | category | flops | bytes accessed | tf_op | source)
XLA Modules:
  0.0 219.0 jit_solution(14530429245393646775)
XLA Ops:
  8.2 1.4 fusion.22
  9.7 1.7 pad_maximum_fusion.1
  11.5 1.6 collective-permute-start.7
  13.9 3.1 %copy.17 = bf16[1,64,2,7168]{3,1,2,0:T(8,128)(2,1)} copy(bf16[1,64,2,7168]{3,2,1,0:T(2,128)(2,1)} %param.13) | data formatting | bytes 3670016 | tf_op args[3]
  17.1 3.7 %fusion.24 = f32[16,64,256]{2,1,0:T(8,128)S(1)} fusion(bf16[16,64,512]{2,1,0:T(8,128)(2,1)S(1)} %copy-done, bf16[16,256,512]{2,1,0:T(8,128)(2,1)} %param.17), kind=kOutput, calls=%fused_computation.58 | convolution fusion | flops 268435456 | bytes 6291456 | tf_op jit(solution)/shard_map/rhc,rlc->rhl/dot_general | solution.py:75
  23.4 5.7 %convolution_convert_fusion = bf16[16,64,512]{2,1,0:T(8,128)(2,1)} fusion(bf16[16,256,512]{2,1,0:T(8,128)(2,1)} %param.17, f32[16,64]{1,0:T(8,128)S(1)} %fusion.23, f32[16,64,256]{2,1,0:T(8,128)} %copy-done.2, pred[16,256]{1,0:T(8,128)(4,1)S(1)} %iota_compare_fusion.1), kind=kOutput, calls=%fused_computation.3 | convolution fusion | flops 270009600 | bytes 6299648 | tf_op jit(solution)/shard_map/rhl,rlc->rhc/dot_general | solution.py:90
  31.9 2.0 collective-permute-done.7
  34.0 1.6 collective-permute-start.9
  38.2 7.0 %collective-permute-done.9 = bf16[32,7168]{1,0:T(8,128)(2,1)S(1)} collective-permute-done((bf16[32,7168]{1,0:T(8,128)(2,1)S(1)}, bf16[32,7168]{1,0:T(8,128)(2,1)S(1)}, u32[]{:S(2)}, u32[]{:S(2)}) %collective-permute-start.9) | collective-permute-done | bytes 458784 | tf_op jit(solution)/shard_map/ppermute | solution.py:38
  47.9 1.3 collective-permute-start
  50.0 2.2 collective-permute-start.1
  52.2 19.1 %collective-permute-done.refs_1_ = bf16[64,7168]{1,0:T(8,128)(2,1)} collective-permute-done((bf16[64,7168]{1,0:T(8,128)(2,1)S(1)}, bf16[64,7168]{1,0:T(8,128)(2,1)}, u32[]{:S(2)}, u32[]{:S(2)}) %collective-permute-start) | collective-permute-done | bytes 917536 | tf_op jit(solution)/shard_map/ppermute | solution.py:38
  71.2 1.2 collective-permute-start.2
  73.4 18.7 %collective-permute-done.1.refs_2_ = bf16[64,7168]{1,0:T(8,128)(2,1)} collective-permute-done((bf16[64,7168]{1,0:T(8,128)(2,1)S(1)}, bf16[64,7168]{1,0:T(8,128)(2,1)}, u32[]{:S(2)}, u32[]{:S(2)}) %collective-permute-start.1) | collective-permute-done | bytes 917536 | tf_op jit(solution)/shard_map/ppermute | solution.py:38
  92.1 18.0 %collective-permute-done.2.refs_3_ = bf16[64,7168]{1,0:T(8,128)(2,1)} collective-permute-done((bf16[64,7168]{1,0:T(8,128)(2,1)}, bf16[64,7168]{1,0:T(8,128)(2,1)}, u32[]{:S(2)}, u32[]{:S(2)}) %collective-permute-start.2) | collective-permute-done | bytes 917536 | tf_op jit(solution)/shard_map/ppermute | solution.py:38
  111.1 13.6 %hidden_units.1.mine_ref = bf16[2,512,256]{2,1,0:T(8,128)(2,1)S(1)} custom-call(s32[1]{0:T(128)} %bitcast.2.expert_ref, bf16[1024,7296]{1,0:T(8,128)(2,1)} %all-gather.2.cloned.1.call-done.x_ref, bf16[64,7168]{1,0:T(8,128)(2,1)S(1)} %get-tuple-element.11.refs_0_, bf16[64,7168]{1,0:T(8,128)(2,1)} %collective-permute-done.refs_1_, ...), custom_call_target="tpu_custom_call" | custom-call | flops 7516192768 | bytes 22282240 | tf_op jit(solution)/shard_map/hidden_units/pallas_call | solution.py:147
  124.9 1.4 collective-permute-done.6.recv_ref
  126.3 6.5 %project.3 = bf16[512,3840]{1,0:T(8,128)(2,1)} custom-call(s32[2]{0:T(128)S(1)} %pad_add_fusion.place_ref, bf16[2,512,256]{2,1,0:T(8,128)(2,1)S(1)} %hidden_units.1.mine_ref, bf16[512,256]{1,0:T(8,128)(2,1)S(1)} %collective-permute-done.6.recv_ref, bf16[256,7168]{1,0:T(8,128)(2,1)} %constant_dynamic-update-slice_fusion.own_ref, ...), custom_call_target="tpu_custom_call" | custom-call | flops 2013265920 | bytes 8388608 | tf_op jit(solution)/shard_map/project/pallas_call | solution.py:209
  132.8 5.3 %project.2 = (bf16[128,3328]{1,0:T(8,128)(2,1)S(1)}, bf16[128,3328]{1,0:T(8,128)(2,1)S(1)}, bf16[128,3328]{1,0:T(8,128)(2,1)S(1)}, bf16[128,3328]{1,0:T(8,128)(2,1)}) custom-call(s32[2]{0:T(128)S(1)} %pad_add_fusion.place_ref, bf16[2,512,256]{2,1,0:T(8,128)(2,1)S(1)} %hidden_units.1.mine_ref, bf16[512,256]{1,0:T(8,128)(2,1)S(1)} %collective-permute-done.6.recv_ref, ...), custom_call_target="tpu_custom_call" | custom-call | flops 1744830464 | bytes 7340032 | tf_op jit(solution)/shard_map/project/pallas_call | solution.py:209
  138.2 2.7 %collective-permute-start.12 = (bf16[128,1664]{1,0:T(8,128)(2,1)S(1)}, bf16[128,1664]{1,0:T(8,128)(2,1)S(1)}, u32[]{:S(2)}, u32[]{:S(2)}) collective-permute-start(bf16[128,1664]{1,0:T(8,128)(2,1)S(1)} %get-tuple-element.14), channel_id=1, source_target_pairs={{0,8},{1,9},{128,136},{129,137},{2,10},{3,11},{130,138},{131,139},... | collective-permute-start | bytes 1277960 | tf_op jit(solution)/shard_map/ppermute | solution.py:38
  142.0 1.7 collective-permute-start.14
  143.7 1.9 collective-permute-start.16
  145.8 7.2 %collective-permute-done.12 = bf16[128,1664]{1,0:T(8,128)(2,1)S(1)} collective-permute-done((bf16[128,1664]{1,0:T(8,128)(2,1)S(1)}, bf16[128,1664]{1,0:T(8,128)(2,1)S(1)}, u32[]{:S(2)}, u32[]{:S(2)}) %collective-permute-start.12) | collective-permute-done | bytes 426016 | tf_op jit(solution)/shard_map/ppermute | solution.py:38
  153.8 9.0 %collective-permute-done.16 = bf16[128,1664]{1,0:T(8,128)(2,1)S(1)} collective-permute-done((bf16[128,1664]{1,0:T(8,128)(2,1)S(1)}, bf16[128,1664]{1,0:T(8,128)(2,1)S(1)}, u32[]{:S(2)}, u32[]{:S(2)}) %collective-permute-start.16) | collective-permute-done | bytes 426016 | tf_op jit(solution)/shard_map/ppermute | solution.py:38
  162.8 3.2 %collective-permute-start.17 = (bf16[128,1664]{1,0:T(8,128)(2,1)S(1)}, bf16[128,1664]{1,0:T(8,128)(2,1)S(1)}, u32[]{:S(2)}, u32[]{:S(2)}) collective-permute-start(bf16[128,1664]{1,0:T(8,128)(2,1)S(1)} %add_convert_fusion.1), channel_id=1, source_target_pairs={{0,24},{1,25},{128,152},{129,153},{2,26},{3,27},{130,154},{131,155... | collective-permute-start | bytes 1277960 | tf_op jit(solution)/shard_map/ppermute | solution.py:38
  166.1 4.8 %collective-permute-done.13 = bf16[128,1664]{1,0:T(8,128)(2,1)S(1)} collective-permute-done((bf16[128,1664]{1,0:T(8,128)(2,1)S(1)}, bf16[128,1664]{1,0:T(8,128)(2,1)S(1)}, u32[]{:S(2)}, u32[]{:S(2)}) %collective-permute-start.13) | collective-permute-done | bytes 426016 | tf_op jit(solution)/shard_map/ppermute | solution.py:38
  170.8 3.9 %collective-permute-done.17 = bf16[128,1664]{1,0:T(8,128)(2,1)S(1)} collective-permute-done((bf16[128,1664]{1,0:T(8,128)(2,1)S(1)}, bf16[128,1664]{1,0:T(8,128)(2,1)S(1)}, u32[]{:S(2)}, u32[]{:S(2)}) %collective-permute-start.17) | collective-permute-done | bytes 426016 | tf_op jit(solution)/shard_map/ppermute | solution.py:38
  176.0 8.2 %all-to-all-start = ((bf16[8,16,3328]{2,1,0:T(8,128)(2,1)}), bf16[8,16,3328]{2,1,0:T(8,128)(2,1)S(1)}, u32[]{:S(2)}, u32[]{:S(2)}) async-start(bf16[8,16,3328]{2,1,0:T(8,128)(2,1)} %bitcast.12), calls=%async_computation | async-start | bytes 1703936 | tf_op jit(solution)/shard_map/all_to_all | solution.py:69
  184.2 13.4 %reduce-scatter.2.cloned.1.call-done = bf16[64,3840]{1,0:T(8,128)(2,1)} async-done(((bf16[512,3840]{1,0:T(8,128)(2,1)}), bf16[64,3840]{1,0:T(8,128)(2,1)}) %reduce-scatter.2.cloned.1.call-update) | async-done | bytes 491536 | tf_op jit(solution)/shard_map/reduce_scatter | solution.py:290
  199.0 5.0 %collective-permute-start.19 = (bf16[16,3840]{1,0:T(8,128)(2,1)S(1)}, bf16[16,3840]{1,0:T(8,128)(2,1)S(1)}, u32[]{:S(2)}, u32[]{:S(2)}) collective-permute-start(bf16[16,3840]{1,0:T(8,128)(2,1)S(1)} %get-tuple-element.18), channel_id=1, source_target_pairs={{0,16},{1,17},{128,144},{129,145},{2,18},{3,19},{130,146},{131,147... | collective-permute-start | bytes 368648 | tf_op jit(solution)/shard_map/ppermute | solution.py:38
  204.0 1.2 collective-permute-start.18
  205.2 5.1 %all-to-all-done = bf16[8,16,3328]{2,1,0:T(8,128)(2,1)S(1)} async-done(((bf16[8,16,3328]{2,1,0:T(8,128)(2,1)}), bf16[8,16,3328]{2,1,0:T(8,128)(2,1)S(1)}, u32[]{:S(2)}, u32[]{:S(2)}) %all-to-all-start) | async-done | bytes 852000 | tf_op jit(solution)/shard_map/all_to_all | solution.py:69
  (72 shorter events, 21.1 us)
Async XLA Ops:
  7.2 9.9 %copy-start = (bf16[16,64,512]{2,1,0:T(8,128)(2,1)S(1)}, bf16[16,64,512]{2,1,0:T(8,128)(2,1)}, u32[]{:S(2)}) copy-start(bf16[16,64,512]{2,1,0:T(8,128)(2,1)} %param.15) | copy-start | bytes 3145732
  7.2 9.8 %copy-start.7 = (s32[16]{0:T(128)S(1)}, s32[16]{0:T(128)}, u32[]{:S(2)}) copy-start(s32[16]{0:T(128)} %param.19) | copy-start | bytes 196
  7.2 103.9 %all-gather.2.cloned.1.call-start = ((), (), s32[]{:S(2)}) async-start(), calls=%async_computation.2 | async-start | bytes 15175680 | tf_op jit(solution)/shard_map/all_gather | solution.py:259
  11.4 186.2 %reduce-scatter.2.cloned.1.call-start = ((), (), s32[]{:S(2)}) async-start(), calls=%async_computation.3 | async-start | bytes 4423680 | tf_op jit(solution)/shard_map/reduce_scatter | solution.py:290
  11.5 22.4 %collective-permute-start.7 = (bf16[64,7168]{1,0:T(8,128)(2,1)}, bf16[64,7168]{1,0:T(8,128)(2,1)S(1)}, u32[]{:S(2)}, u32[]{:S(2)}) collective-permute-start(bf16[64,7168]{1,0:T(8,128)(2,1)} %bitcast.40), channel_id=1, source_target_pairs={{0,32},{1,33},{128,160},{129,161},{2,34},{3,35},{130,162},{131,163... | collective-permute-start | bytes 2752520 | tf_op jit(solution)/shard_map/ppermute | solution.py:38
  13.0 22.5 %collective-permute-start.8 = (bf16[64,7168]{1,0:T(8,128)(2,1)}, bf16[64,7168]{1,0:T(8,128)(2,1)S(1)}, u32[]{:S(2)}, u32[]{:S(2)}) collective-permute-start(bf16[64,7168]{1,0:T(8,128)(2,1)} %bitcast.41), channel_id=1, source_target_pairs={{0,96},{1,97},{128,224},{129,225},{2,98},{3,99},{130,226},{131,227... | collective-permute-start | bytes 2752520 | tf_op jit(solution)/shard_map/ppermute | solution.py:38
  17.0 3.8 %copy-start.3 = (bf16[1,64,7168]{2,1,0:T(8,128)(2,1)S(1)}, bf16[1,64,7168]{2,1,0:T(8,128)(2,1)}, u32[]{:S(2)}) copy-start(bf16[1,64,7168]{2,1,0:T(8,128)(2,1)} %param.14) | copy-start | bytes 2752516
  17.1 4.7 %copy-start.5 = (bf16[16,64,256]{2,1,0:T(8,128)(2,1)S(1)}, bf16[16,64,256]{2,1,0:T(8,128)(2,1)}, u32[]{:S(2)}) copy-start(bf16[16,64,256]{2,1,0:T(8,128)(2,1)} %param.18) | copy-start | bytes 1572868
  17.1 4.7 %copy-start.6 = (bf16[16,64,64]{2,1,0:T(8,128)(2,1)S(1)}, bf16[16,64,64]{2,1,0:T(8,128)(2,1)}, u32[]{:S(2)}) copy-start(bf16[16,64,64]{2,1,0:T(8,128)(2,1)} %param.16) | copy-start | bytes 393220
  22.1 1.0 copy-start.2
  31.8 15.9 %copy-start.1 = (bf16[1,64,2,7168]{3,1,2,0:T(8,128)(2,1)S(1)}, bf16[1,64,2,7168]{3,1,2,0:T(8,128)(2,1)}, u32[]{:S(2)}) copy-start(bf16[1,64,2,7168]{3,1,2,0:T(8,128)(2,1)} %copy.17) | copy-start | bytes 5505028
  34.0 11.3 %collective-permute-start.9 = (bf16[32,7168]{1,0:T(8,128)(2,1)S(1)}, bf16[32,7168]{1,0:T(8,128)(2,1)S(1)}, u32[]{:S(2)}, u32[]{:S(2)}) collective-permute-start(bf16[32,7168]{1,0:T(8,128)(2,1)S(1)} %constant_dynamic-slice_fusion.1), channel_id=1, source_target_pairs={{0,32},{1,33},{128,160},{129,161},{2,34},{3,35},{130,162},{131,163... | collective-permute-start | bytes 1376264 | tf_op jit(solution)/shard_map/ppermute | solution.py:38
  35.6 11.3 %collective-permute-start.10 = (bf16[32,7168]{1,0:T(8,128)(2,1)S(1)}, bf16[32,7168]{1,0:T(8,128)(2,1)S(1)}, u32[]{:S(2)}, u32[]{:S(2)}) collective-permute-start(bf16[32,7168]{1,0:T(8,128)(2,1)S(1)} %constant_dynamic-slice_fusion), channel_id=1, source_target_pairs={{0,96},{1,97},{128,224},{129,225},{2,98},{3,99},{130,226},{131,227... | collective-permute-start | bytes 1376264 | tf_op jit(solution)/shard_map/ppermute | solution.py:38
  47.8 77.1 %collective-permute-start.11 = (bf16[256,7168]{1,0:T(8,128)(2,1)}, bf16[256,7168]{1,0:T(8,128)(2,1)}, u32[]{:S(2)}, u32[]{:S(2)}) collective-permute-start(bf16[256,7168]{1,0:T(8,128)(2,1)} %constant_dynamic-update-slice_fusion.own_ref), channel_id=1, source_target_pairs={{0,1},{1,0},{128,129},{129,128},{2,3},{3,2},{130,131},{131,130},{4... | collective-permute-start | bytes 11010056 | tf_op jit(solution)/shard_map/ppermute | solution.py:38
  47.9 23.3 %collective-permute-start = (bf16[64,7168]{1,0:T(8,128)(2,1)S(1)}, bf16[64,7168]{1,0:T(8,128)(2,1)}, u32[]{:S(2)}, u32[]{:S(2)}) collective-permute-start(bf16[64,7168]{1,0:T(8,128)(2,1)S(1)} %get-tuple-element.11.refs_0_), channel_id=1, source_target_pairs={{0,32},{1,33},{128,160},{129,161},{2,34},{3,35},{130,162},{131,163... | collective-permute-start | bytes 2752520 | tf_op jit(solution)/shard_map/ppermute | solution.py:38
  49.2 23.3 %collective-permute-start.4 = (bf16[64,7168]{1,0:T(8,128)(2,1)S(1)}, bf16[64,7168]{1,0:T(8,128)(2,1)}, u32[]{:S(2)}, u32[]{:S(2)}) collective-permute-start(bf16[64,7168]{1,0:T(8,128)(2,1)S(1)} %get-tuple-element.10.refs_4_), channel_id=1, source_target_pairs={{0,96},{1,97},{128,224},{129,225},{2,98},{3,99},{130,226},{131,227... | collective-permute-start | bytes 2752520 | tf_op jit(solution)/shard_map/ppermute | solution.py:38
  50.0 42.1 %collective-permute-start.1 = (bf16[64,7168]{1,0:T(8,128)(2,1)S(1)}, bf16[64,7168]{1,0:T(8,128)(2,1)}, u32[]{:S(2)}, u32[]{:S(2)}) collective-permute-start(bf16[64,7168]{1,0:T(8,128)(2,1)S(1)} %get-tuple-element.11.refs_0_), channel_id=1, source_target_pairs={{0,96},{1,97},{128,224},{129,225},{2,98},{3,99},{130,226},{131,227... | collective-permute-start | bytes 2752520 | tf_op jit(solution)/shard_map/ppermute | solution.py:38
  52.2 40.0 %collective-permute-start.3 = (bf16[64,7168]{1,0:T(8,128)(2,1)S(1)}, bf16[64,7168]{1,0:T(8,128)(2,1)}, u32[]{:S(2)}, u32[]{:S(2)}) collective-permute-start(bf16[64,7168]{1,0:T(8,128)(2,1)S(1)} %get-tuple-element.10.refs_4_), channel_id=1, source_target_pairs={{0,32},{1,33},{128,160},{129,161},{2,34},{3,35},{130,162},{131,163... | collective-permute-start | bytes 2752520 | tf_op jit(solution)/shard_map/ppermute | solution.py:38
  71.2 38.9 %collective-permute-start.2 = (bf16[64,7168]{1,0:T(8,128)(2,1)}, bf16[64,7168]{1,0:T(8,128)(2,1)}, u32[]{:S(2)}, u32[]{:S(2)}) collective-permute-start(bf16[64,7168]{1,0:T(8,128)(2,1)} %collective-permute-done.refs_1_), channel_id=1, source_target_pairs={{0,32},{1,33},{128,160},{129,161},{2,34},{3,35},{130,162},{131,163... | collective-permute-start | bytes 2752520 | tf_op jit(solution)/shard_map/ppermute | solution.py:38
  72.5 38.6 %collective-permute-start.5 = (bf16[64,7168]{1,0:T(8,128)(2,1)}, bf16[64,7168]{1,0:T(8,128)(2,1)}, u32[]{:S(2)}, u32[]{:S(2)}) collective-permute-start(bf16[64,7168]{1,0:T(8,128)(2,1)} %collective-permute-done.4.refs_6_), channel_id=1, source_target_pairs={{0,96},{1,97},{128,224},{129,225},{2,98},{3,99},{130,226},{131,227... | collective-permute-start | bytes 2752520 | tf_op jit(solution)/shard_map/ppermute | solution.py:38
  124.7 1.6 collective-permute-start.6
  138.1 24.6 %copy-start.4 = (bf16[128,3328]{1,0:T(8,128)(2,1)S(1)}, bf16[128,3328]{1,0:T(8,128)(2,1)}, u32[]{:S(2)}) copy-start(bf16[128,3328]{1,0:T(8,128)(2,1)} %get-tuple-element.9) | copy-start | bytes 2555908
  138.2 14.8 %collective-permute-start.12 = (bf16[128,1664]{1,0:T(8,128)(2,1)S(1)}, bf16[128,1664]{1,0:T(8,128)(2,1)S(1)}, u32[]{:S(2)}, u32[]{:S(2)}) collective-permute-start(bf16[128,1664]{1,0:T(8,128)(2,1)S(1)} %get-tuple-element.14), channel_id=1, source_target_pairs={{0,8},{1,9},{128,136},{129,137},{2,10},{3,11},{130,138},{131,139},... | collective-permute-start | bytes 1277960 | tf_op jit(solution)/shard_map/ppermute | solution.py:38
  142.0 24.1 %collective-permute-start.14 = (bf16[128,1664]{1,0:T(8,128)(2,1)S(1)}, bf16[128,1664]{1,0:T(8,128)(2,1)S(1)}, u32[]{:S(2)}, u32[]{:S(2)}) collective-permute-start(bf16[128,1664]{1,0:T(8,128)(2,1)S(1)} %slice.43), channel_id=1, source_target_pairs={{0,24},{1,25},{128,152},{129,153},{2,26},{3,27},{130,154},{131,155... | collective-permute-start | bytes 1277960 | tf_op jit(solution)/shard_map/ppermute | solution.py:38
  143.7 19.1 %collective-permute-start.16 = (bf16[128,1664]{1,0:T(8,128)(2,1)S(1)}, bf16[128,1664]{1,0:T(8,128)(2,1)S(1)}, u32[]{:S(2)}, u32[]{:S(2)}) collective-permute-start(bf16[128,1664]{1,0:T(8,128)(2,1)S(1)} %get-tuple-element.15), channel_id=1, source_target_pairs={{0,24},{1,25},{128,152},{129,153},{2,26},{3,27},{130,154},{131,155... | collective-permute-start | bytes 1277960 | tf_op jit(solution)/shard_map/ppermute | solution.py:38
  145.6 20.4 %collective-permute-start.15 = (bf16[128,1664]{1,0:T(8,128)(2,1)S(1)}, bf16[128,1664]{1,0:T(8,128)(2,1)S(1)}, u32[]{:S(2)}, u32[]{:S(2)}) collective-permute-start(bf16[128,1664]{1,0:T(8,128)(2,1)S(1)} %slice.45), channel_id=1, source_target_pairs={{0,8},{1,9},{128,136},{129,137},{2,10},{3,11},{130,138},{131,139},... | collective-permute-start | bytes 1277960 | tf_op jit(solution)/shard_map/ppermute | solution.py:38
  153.2 17.7 %collective-permute-start.13 = (bf16[128,1664]{1,0:T(8,128)(2,1)S(1)}, bf16[128,1664]{1,0:T(8,128)(2,1)S(1)}, u32[]{:S(2)}, u32[]{:S(2)}) collective-permute-start(bf16[128,1664]{1,0:T(8,128)(2,1)S(1)} %add_convert_fusion.3), channel_id=1, source_target_pairs={{0,8},{1,9},{128,136},{129,137},{2,10},{3,11},{130,138},{131,139},... | collective-permute-start | bytes 1277960 | tf_op jit(solution)/shard_map/ppermute | solution.py:38
  162.8 11.8 %collective-permute-start.17 = (bf16[128,1664]{1,0:T(8,128)(2,1)S(1)}, bf16[128,1664]{1,0:T(8,128)(2,1)S(1)}, u32[]{:S(2)}, u32[]{:S(2)}) collective-permute-start(bf16[128,1664]{1,0:T(8,128)(2,1)S(1)} %add_convert_fusion.1), channel_id=1, source_target_pairs={{0,24},{1,25},{128,152},{129,153},{2,26},{3,27},{130,154},{131,155... | collective-permute-start | bytes 1277960 | tf_op jit(solution)/shard_map/ppermute | solution.py:38
  176.0 34.3 %all-to-all-start = ((bf16[8,16,3328]{2,1,0:T(8,128)(2,1)}), bf16[8,16,3328]{2,1,0:T(8,128)(2,1)S(1)}, u32[]{:S(2)}, u32[]{:S(2)}) async-start(bf16[8,16,3328]{2,1,0:T(8,128)(2,1)} %bitcast.12), calls=%async_computation | async-start | bytes 1703936 | tf_op jit(solution)/shard_map/all_to_all | solution.py:69
  198.7 11.7 %collective-permute-start.20 = (bf16[16,3840]{1,0:T(8,128)(2,1)S(1)}, bf16[16,3840]{1,0:T(8,128)(2,1)S(1)}, u32[]{:S(2)}, u32[]{:S(2)}) collective-permute-start(bf16[16,3840]{1,0:T(8,128)(2,1)S(1)} %get-tuple-element.17), channel_id=1, source_target_pairs={{0,24},{1,25},{128,152},{129,153},{2,26},{3,27},{130,154},{131,155... | collective-permute-start | bytes 368648 | tf_op jit(solution)/shard_map/ppermute | solution.py:38
  199.0 11.4 %collective-permute-start.19 = (bf16[16,3840]{1,0:T(8,128)(2,1)S(1)}, bf16[16,3840]{1,0:T(8,128)(2,1)S(1)}, u32[]{:S(2)}, u32[]{:S(2)}) collective-permute-start(bf16[16,3840]{1,0:T(8,128)(2,1)S(1)} %get-tuple-element.18), channel_id=1, source_target_pairs={{0,16},{1,17},{128,144},{129,145},{2,18},{3,19},{130,146},{131,147... | collective-permute-start | bytes 368648 | tf_op jit(solution)/shard_map/ppermute | solution.py:38
  204.0 6.4 %collective-permute-start.18 = (bf16[16,3840]{1,0:T(8,128)(2,1)S(1)}, bf16[16,3840]{1,0:T(8,128)(2,1)S(1)}, u32[]{:S(2)}, u32[]{:S(2)}) collective-permute-start(bf16[16,3840]{1,0:T(8,128)(2,1)S(1)} %get-tuple-element.16), channel_id=1, source_target_pairs={{0,8},{1,9},{128,136},{129,137},{2,10},{3,11},{130,138},{131,139},... | collective-permute-start | bytes 368648 | tf_op jit(solution)/shard_map/ppermute | solution.py:38
Sparse Core Ops, SparseCore 0:
  11.5 98.2 all-gather.1
  133.0 64.6 reduce-scatter.1
